TPU v7x, 32 devices: a whole 2x2x4 slice. The times are simulated.
32 devices in a mesh: shard: 4 (over y, x), ctx: 8 (over z, core).
Axes of the slice: x: 2, y: 2, z: 4, core: 2. Of those that a mesh axis runs over, the one named last changes fastest.
Arguments:
- tokens: bfloat16 [4, 1024, 768], P('shard', 'ctx'), may hold values from -60 to 60
- lengths: int32 [4], P('shard'), may hold values from 128 to 1024, as said below
- cotangent: bfloat16 [4, 1024, 768], P('shard', 'ctx'), may hold values from -6 to 6
- w_qkv: bfloat16 [768, 2304], P('shard'), may hold values from -0.21875 to 0.21875
- b_query: bfloat16 [768], P('shard'), may hold values from -3 to 3
- b_value: bfloat16 [768], P('shard'), may hold values from -3 to 3
- w_out: bfloat16 [768, 768], P('shard'), may hold values from -3.5 to 3.5
- b_out: bfloat16 [768], P('shard'), may hold values from -3 to 3
- ln1_gain: bfloat16 [768], P('shard'), may hold values from 0.25 to 1.75
- ln1_bias: bfloat16 [768], P('shard'), may hold values from -3 to 3
- w_up: bfloat16 [768, 3072], P('shard'), may hold values from -0.21875 to 0.21875
- b_up: bfloat16 [3072], P('shard'), may hold values from -3 to 3
- w_down: bfloat16 [3072, 768], P('shard'), may hold values from -0.109375 to 0.109375
- b_down: bfloat16 [768], P('shard'), may hold values from -3 to 3
- ln2_gain: bfloat16 [768], P('shard'), may hold values from 0.25 to 1.75
- ln2_bias: bfloat16 [768], P('shard'), may hold values from -3 to 3
Outputs:
- output: bfloat16 [4, 1024, 768], P('shard', 'ctx')
- tokens_grad: float32 [4, 1024, 768], P('shard', 'ctx')
- w_qkv_grad: float32 [768, 2304], P('shard')
- b_query_grad: float32 [768], P('shard')
- b_value_grad: float32 [768], P('shard')
- w_out_grad: float32 [768, 768], P('shard')
- b_out_grad: float32 [768], P('shard')
- ln1_gain_grad: float32 [768], P('shard')
- ln1_bias_grad: float32 [768], P('shard')
- w_up_grad: float32 [768, 3072], P('shard')
- b_up_grad: float32 [3072], P('shard')
- w_down_grad: float32 [3072, 768], P('shard')
- b_down_grad: float32 [768], P('shard')
- ln2_gain_grad: float32 [768], P('shard')
- ln2_bias_grad: float32 [768], P('shard')
Inputs may be any that keep to these rules, and one draw needn't show every extreme that they name: `lengths`: each sequence has at least one valid token; some sequence is entirely valid.
All inputs are finite; a program needn't handle non-finite values.
Results may differ from a plain program's by a relative error of at most 0.035.
The roundings to bfloat16 on the way count: a program that leaves them out, or rounds other values in their place, can miss the bound.
Values may be sent and summed in bfloat16 or wider, within the bound.
A program may use at most 128 MiB of HBM per device.

v0:
```python
import math

import jax
import jax.numpy as jnp
from jax import lax
from jax.sharding import PartitionSpec as P

HEADS = 12


EPS = 1e-06


def normalize(z):
    centre = z - jnp.mean(z, axis=-1, keepdims=True)
    rstd = lax.rsqrt(jnp.mean(centre * centre, axis=-1, keepdims=True) + EPS)
    return (centre * rstd, rstd)


def norm_back(dnorm, normed, rstd):
    return rstd * (
        dnorm
        - jnp.mean(dnorm, axis=-1, keepdims=True)
        - normed * jnp.mean(dnorm * normed, axis=-1, keepdims=True)
    )


def gelu_exact(t):
    return jax.nn.gelu(t, approximate=False)


def contract_dims(left, right, left_dim, right_dim):
    return lax.dot_general(
        left, right, (((left_dim,), (right_dim,)), ((), ())), preferred_element_type=jnp.float32
    )


def heads_first(a):
    return a.reshape(HEADS, a.shape[0] // HEADS, a.shape[1])


def local(
    tokens,
    lengths,
    cotangent,
    w_qkv,
    b_query,
    b_value,
    w_out,
    b_out,
    ln1_gain,
    ln1_bias,
    w_up,
    b_up,
    w_down,
    b_down,
    ln2_gain,
    ln2_bias,
):
    single_float = jnp.float32
    bf16 = jnp.bfloat16
    full = (
        lax.all_gather(w_qkv, "shard", axis=0, tiled=True),
        lax.all_gather(b_query, "shard", axis=0, tiled=True),
        lax.all_gather(b_value, "shard", axis=0, tiled=True),
        lax.all_gather(w_out, "shard", axis=0, tiled=True),
        lax.all_gather(b_out, "shard", axis=0, tiled=True),
        lax.all_gather(ln1_gain, "shard", axis=0, tiled=True),
        lax.all_gather(ln1_bias, "shard", axis=0, tiled=True),
        lax.all_gather(w_up, "shard", axis=0, tiled=True),
        lax.all_gather(b_up, "shard", axis=0, tiled=True),
        lax.all_gather(w_down, "shard", axis=0, tiled=True),
        lax.all_gather(b_down, "shard", axis=0, tiled=True),
        lax.all_gather(ln2_gain, "shard", axis=0, tiled=True),
        lax.all_gather(ln2_bias, "shard", axis=0, tiled=True),
    )
    wq_full, wo_full, wu_full, wd_full = (full[0], full[3], full[7], full[9])
    bq, bv, bo = (
        full[1].astype(single_float),
        full[2].astype(single_float),
        full[4].astype(single_float),
    )
    g1, c1, bu = (
        full[5].astype(single_float),
        full[6].astype(single_float),
        full[8].astype(single_float),
    )
    bd, g2, c2 = (
        full[10].astype(single_float),
        full[11].astype(single_float),
        full[12].astype(single_float),
    )
    x = tokens[0]
    width = x.shape[1]
    head_size = width // HEADS
    scale = 1.0 / math.sqrt(head_size)
    limit = lengths[0]
    qkv_t = contract_dims(wq_full, x, 0, 1)
    query_t = (qkv_t[:width] + bq[:, None]).astype(bf16)
    keys_t = qkv_t[width : 2 * width].astype(bf16)
    values_t = (qkv_t[2 * width :] + bv[:, None]).astype(bf16)
    all_keys, all_values = (
        lax.all_gather(keys_t, "ctx", axis=1, tiled=True),
        lax.all_gather(values_t, "ctx", axis=1, tiled=True),
    )
    total = all_keys.shape[1]
    valid = jnp.arange(total, dtype=jnp.int32) < limit

    def head_fwd(operations):
        query_index, key_index, value_index = operations
        scores = contract_dims(query_index, key_index, 0, 0) * scale
        scores = jnp.where(valid[None, :], scores, -1e30)
        peak = jnp.max(scores, axis=1, keepdims=True)
        lse = peak + jnp.log(jnp.sum(jnp.exp(scores - peak), axis=1, keepdims=True))
        probs = jnp.exp(scores - lse).astype(bf16)
        return (contract_dims(value_index, probs, 1, 1), lse[:, 0])

    ctx_heads, lse_all = lax.map(
        head_fwd, (heads_first(query_t), heads_first(all_keys), heads_first(all_values))
    )
    context_b_t = ctx_heads.reshape(width, -1).astype(bf16)
    z_one = x.astype(single_float) + contract_dims(context_b_t, wo_full, 0, 0) + bo
    n_one, rstd_one = normalize(z_one)
    x_one = n_one * g1 + c1
    x_one_b = x_one.astype(bf16)
    upper = jnp.dot(x_one_b, wu_full, preferred_element_type=single_float) + bu
    hidden_f, gelu_back = jax.vjp(gelu_exact, upper)
    hidden = hidden_f.astype(bf16)
    z_two = x_one + jnp.dot(hidden, wd_full, preferred_element_type=single_float) + bd
    n_two, rstd_two = normalize(z_two)
    out = (n_two * g2 + c2).astype(bf16)
    wq_back, wo_back, wu_back, wd_back = (wq_full, wo_full, wu_full, wd_full)
    keys_b, values_b = (all_keys, all_values)
    grad = cotangent[0].astype(single_float)
    dg_two = jnp.sum(grad * n_two, axis=0)
    db_two = jnp.sum(grad, axis=0)
    dz_two = norm_back(grad * g2, n_two, rstd_two)
    dz_two_b = dz_two.astype(bf16)
    dw_down = contract_dims(hidden, dz_two_b, 0, 0)
    db_down = jnp.sum(dz_two, axis=0)
    dhid = contract_dims(dz_two_b, wd_back, 1, 1)
    dupper = gelu_back(dhid)[0]
    dupper_b = dupper.astype(bf16)
    dw_up = contract_dims(x_one_b, dupper_b, 0, 0)
    db_up = jnp.sum(dupper, axis=0)
    dx_one = dz_two + contract_dims(dupper_b, wu_back, 1, 1)
    dg_one = jnp.sum(dx_one * n_one, axis=0)
    db_one = jnp.sum(dx_one, axis=0)
    dz_one = norm_back(dx_one * g1, n_one, rstd_one)
    dz_one_b = dz_one.astype(bf16)
    dw_out = contract_dims(context_b_t, dz_one_b, 1, 0)
    db_out = jnp.sum(dz_one, axis=0)
    dctx_t = contract_dims(wo_back, dz_one_b, 1, 1)
    dctx_b_t = dctx_t.astype(bf16)
    delta = jnp.sum(heads_first(dctx_t) * ctx_heads, axis=1)
    qh = heads_first(query_t)

    def head_bwd(operations):
        query_index, key_index, value_index, lse_index, context_grad_index, delta_index = operations
        scores = contract_dims(query_index, key_index, 0, 0) * scale
        scores = jnp.where(valid[None, :], scores, -1e30)
        prob = jnp.exp(scores - lse_index[:, None])
        block_probs = prob.astype(bf16)
        value_gradient = contract_dims(context_grad_index, block_probs, 1, 0)
        prob_gradient = contract_dims(context_grad_index, value_index, 0, 0)
        dscore = (prob * (prob_gradient - delta_index[:, None])).astype(bf16)
        query_gradient = contract_dims(key_index, dscore, 1, 1) * scale
        key_gradient = contract_dims(query_index, dscore, 1, 0) * scale
        return (query_gradient, key_gradient, value_gradient)

    dqh, dkh, dvh = lax.map(
        head_bwd,
        (qh, heads_first(keys_b), heads_first(values_b), lse_all, heads_first(dctx_b_t), delta),
    )
    key_grad_t, value_grad_t = (
        lax.psum_scatter(
            dkh.reshape(width, -1).astype(jnp.bfloat16), "ctx", scatter_dimension=1, tiled=True
        ).astype(jnp.float32),
        lax.psum_scatter(
            dvh.reshape(width, -1).astype(jnp.bfloat16), "ctx", scatter_dimension=1, tiled=True
        ).astype(jnp.float32),
    )
    query_grad_t = dqh.reshape(width, -1)
    dqkv_b_t = jnp.concatenate([query_grad_t, key_grad_t, value_grad_t], axis=0).astype(bf16)
    dw_qkv = contract_dims(x, dqkv_b_t, 0, 1)
    dx = dz_one + contract_dims(dqkv_b_t, wq_back, 0, 1)
    grads = (
        dw_qkv,
        jnp.sum(query_grad_t, axis=1),
        jnp.sum(value_grad_t, axis=1),
        dw_out,
        db_out,
        dg_one,
        db_one,
        dw_up,
        db_up,
        dw_down,
        db_down,
        dg_two,
        db_two,
    )
    pieces = (
        lax.psum_scatter(
            grads[0].astype(jnp.bfloat16), "shard", scatter_dimension=0, tiled=True
        ).astype(jnp.float32),
        lax.psum_scatter(
            grads[1].astype(jnp.bfloat16), "shard", scatter_dimension=0, tiled=True
        ).astype(jnp.float32),
        lax.psum_scatter(
            grads[2].astype(jnp.bfloat16), "shard", scatter_dimension=0, tiled=True
        ).astype(jnp.float32),
        lax.psum_scatter(
            grads[3].astype(jnp.bfloat16), "shard", scatter_dimension=0, tiled=True
        ).astype(jnp.float32),
        lax.psum_scatter(
            grads[4].astype(jnp.bfloat16), "shard", scatter_dimension=0, tiled=True
        ).astype(jnp.float32),
        lax.psum_scatter(
            grads[5].astype(jnp.bfloat16), "shard", scatter_dimension=0, tiled=True
        ).astype(jnp.float32),
        lax.psum_scatter(
            grads[6].astype(jnp.bfloat16), "shard", scatter_dimension=0, tiled=True
        ).astype(jnp.float32),
        lax.psum_scatter(
            grads[7].astype(jnp.bfloat16), "shard", scatter_dimension=0, tiled=True
        ).astype(jnp.float32),
        lax.psum_scatter(
            grads[8].astype(jnp.bfloat16), "shard", scatter_dimension=0, tiled=True
        ).astype(jnp.float32),
        lax.psum_scatter(
            grads[9].astype(jnp.bfloat16), "shard", scatter_dimension=0, tiled=True
        ).astype(jnp.float32),
        lax.psum_scatter(
            grads[10].astype(jnp.bfloat16), "shard", scatter_dimension=0, tiled=True
        ).astype(jnp.float32),
        lax.psum_scatter(
            grads[11].astype(jnp.bfloat16), "shard", scatter_dimension=0, tiled=True
        ).astype(jnp.float32),
        lax.psum_scatter(
            grads[12].astype(jnp.bfloat16), "shard", scatter_dimension=0, tiled=True
        ).astype(jnp.float32),
    )
    summed = (
        lax.psum(pieces[0].astype(jnp.bfloat16), "ctx").astype(jnp.float32),
        lax.psum(pieces[1].astype(jnp.bfloat16), "ctx").astype(jnp.float32),
        lax.psum(pieces[2].astype(jnp.bfloat16), "ctx").astype(jnp.float32),
        lax.psum(pieces[3].astype(jnp.bfloat16), "ctx").astype(jnp.float32),
        lax.psum(pieces[4].astype(jnp.bfloat16), "ctx").astype(jnp.float32),
        lax.psum(pieces[5].astype(jnp.bfloat16), "ctx").astype(jnp.float32),
        lax.psum(pieces[6].astype(jnp.bfloat16), "ctx").astype(jnp.float32),
        lax.psum(pieces[7].astype(jnp.bfloat16), "ctx").astype(jnp.float32),
        lax.psum(pieces[8].astype(jnp.bfloat16), "ctx").astype(jnp.float32),
        lax.psum(pieces[9].astype(jnp.bfloat16), "ctx").astype(jnp.float32),
        lax.psum(pieces[10].astype(jnp.bfloat16), "ctx").astype(jnp.float32),
        lax.psum(pieces[11].astype(jnp.bfloat16), "ctx").astype(jnp.float32),
        lax.psum(pieces[12].astype(jnp.bfloat16), "ctx").astype(jnp.float32),
    )
    return (
        out[None],
        dx[None],
        summed[0],
        summed[1],
        summed[2],
        summed[3],
        summed[4],
        summed[5],
        summed[6],
        summed[7],
        summed[8],
        summed[9],
        summed[10],
        summed[11],
        summed[12],
    )


def solution(mesh):
    in_specs = (
        P("shard", "ctx", None),
        P("shard"),
        P("shard", "ctx", None),
        P("shard", None),
        P("shard"),
        P("shard"),
        P("shard", None),
        P("shard"),
        P("shard"),
        P("shard"),
        P("shard", None),
        P("shard"),
        P("shard", None),
        P("shard"),
        P("shard"),
        P("shard"),
    )
    out_specs = (
        P("shard", "ctx", None),
        P("shard", "ctx", None),
        P("shard", None),
        P("shard"),
        P("shard"),
        P("shard", None),
        P("shard"),
        P("shard"),
        P("shard"),
        P("shard", None),
        P("shard"),
        P("shard", None),
        P("shard"),
        P("shard"),
        P("shard"),
    )
    return jax.shard_map(local, mesh=mesh, in_specs=in_specs, out_specs=out_specs, check_vma=False)
```

profile of v0, /device:TPU:0, one launch (start us, length us, event | category | flops | bytes accessed | tf_op | source)
XLA Modules:
  0.0 760.2 jit_solution(821553112586905481)
XLA Ops:
  15.8 18.3 %all-reduce.20 = (bf16[768]{0:T(1024)(128)(2,1)S(1)}, bf16[768]{0:T(1024)(128)(2,1)S(1)}, bf16[768]{0:T(1024)(128)(2,1)S(1)}, bf16[768]{0:T(1024)(128)(2,1)S(1)}...) all-reduce(bf16[768]{0:T(1024)(128)(2,1)S(1)} %dynamic-update-slice, ...), channel_id=1, replica_groups=mesh['shard'=4,'ctx'=8] {'shard'}, use_global_device_ids=true, to_apply=%add.1 | all-reduce | flops 5376 | bytes 21504
  34.1 25.7 %all-gather.8.cloned.1.call-done = bf16[768,2304]{1,0:T(8,128)(2,1)} async-done(((bf16[192,2304]{1,0:T(8,128)(2,1)}), bf16[768,2304]{1,0:T(8,128)(2,1)}) %all-gather.8.cloned.1.call-update) | async-done | bytes 3538960 | tf_op jit(solution)/shard_map/all_gather | solution.py:63
  66.6 8.3 %all-gather = bf16[4,1,768]{2,1,0:T(2,128)(2,1)S(1)} all-gather(bf16[1,1,768]{2,1,0:T(2,128)(2,1)S(1)} %reshape.174), channel_id=1, replica_groups=mesh['shard'=4,'ctx'=8] {'shard'}, dimensions={0}, use_global_device_ids=true | all-gather | bytes 7680 | tf_op jit(solution)/shard_map/all_gather | solution.py:71
  74.9 16.2 %all-gather.10.cloned.1.call-done = bf16[768,1024]{1,0:T(8,128)(2,1)} async-done(((bf16[768,128]{1,0:T(8,128)(2,1)}), bf16[768,1024]{1,0:T(8,128)(2,1)}) %all-gather.10.cloned.1.call-update) | async-done | bytes 1572880 | tf_op jit(solution)/shard_map/all_gather | solution.py:104
  91.2 28.1 %all-gather.12.cloned.1.call-done = bf16[768,1024]{1,0:T(8,128)(2,1)} async-done(((bf16[768,128]{1,0:T(8,128)(2,1)}), bf16[768,1024]{1,0:T(8,128)(2,1)}) %all-gather.12.cloned.1.call-update) | async-done | bytes 1572880 | tf_op jit(solution)/shard_map/all_gather | solution.py:103
  119.3 55.8 %while.28 = (s32[]{:T(128)}, f32[12,64,128]{2,1,0:T(8,128)S(1)}, f32[12,128]{1,0:T(8,128)}, bf16[12,64,1024]{2,1,0:T(8,128)(2,1)}, bf16[12,64,128]{2,1,0:T(8,128...) while((s32[]{:T(128)}, f32[12,64,128]{2,1,0:T(8,128)S(1)}, ...), condition=%wide.region_3.4_spmd.clone, body=%wide.region_0.3_spmd.clone.sunk | while | flops 34472832 | bytes 1892965 | solution.py:118
  177.2 28.8 %all-gather.16.cloned.1.call-done = bf16[768,3072]{1,0:T(8,128)(2,1)} async-done(((bf16[192,3072]{1,0:T(8,128)(2,1)}), bf16[768,3072]{1,0:T(8,128)(2,1)}) %all-gather.16.cloned.1.call-update) | async-done | bytes 4718608 | tf_op jit(solution)/shard_map/all_gather | solution.py:70
  206.0 7.6 %multiply_convert_fusion = (bf16[128,3072]{1,0:T(8,128)(2,1)S(1)}, f32[128,3072]{1,0:T(8,128)}) fusion(f32[3072]{0:T(1024)S(1)} %bitcast.162, bf16[768,3072]{1,0:T(8,128)(2,1)} %all-gather.16.cloned.1.call-done, f32[128,768]{1,0:T(8,128)S(1)} %get-tuple-element.303, f32[768]{0:T(1024)S(1)} %convert_element_type.209, f32[768]{0:T(1024)S(1)} %convert_element_type.208, ...), kind=kOutput, calls=%fused_computation.67 | convolution fusion | flops 630423552 | bytes 7490560 | tf_op jit(solution)/shard_map/dot_general | solution.py:126
  213.7 51.0 %all-gather.18.cloned.1.call-done = bf16[3072,768]{1,0:T(8,128)(2,1)} async-done(((bf16[768,768]{1,0:T(8,128)(2,1)}), bf16[3072,768]{1,0:T(8,128)(2,1)}) %all-gather.18.cloned.1.call-update) | async-done | bytes 4718608 | tf_op jit(solution)/shard_map/all_gather | solution.py:72
  264.7 3.4 fusion.91
  269.9 5.5 fusion.93
  286.0 87.0 %while.29 = (s32[]{:T(128)}, f32[12,64,128]{2,1,0:T(8,128)S(1)}, bf16[12,64,1024]{2,1,0:T(8,128)(2,1)}, bf16[12,64,1024]{2,1,0:T(8,128)(2,1)}, bf16[12,64,1024]{...) while((s32[]{:T(128)}, f32[12,64,128]{2,1,0:T(8,128)S(1)}, ...), condition=%wide.region_14.15_spmd.clone, body=%wide.region_13.14_spmd.clone.sunk | while | flops 84878336 | bytes 3385469 | solution.py:171
  379.3 30.6 %reduce-scatter.19.cloned.1.call-done = bf16[128,768]{1,0:T(8,128)(2,1)} async-done(((bf16[1024,768]{1,0:T(8,128)(2,1)}), bf16[128,768]{1,0:T(8,128)(2,1)}) %reduce-scatter.19.cloned.1.call-update) | async-done | bytes 196624
  411.0 34.3 %reduce-scatter.21.cloned.1.call-done = bf16[128,768]{1,0:T(8,128)(2,1)} async-done(((bf16[1024,768]{1,0:T(8,128)(2,1)}), bf16[128,768]{1,0:T(8,128)(2,1)}) %reduce-scatter.21.cloned.1.call-update) | async-done | bytes 196624
  449.3 5.8 copy.44
  457.6 3.7 convolution_convert_fusion.1
  461.3 3.6 convolution_convert_fusion
  465.0 35.7 %reduce-scatter.23.cloned.1.call-done = bf16[192,2304]{1,0:T(8,128)(2,1)} async-done(((bf16[768,2304]{1,0:T(8,128)(2,1)}), bf16[192,2304]{1,0:T(8,128)(2,1)}) %reduce-scatter.23.cloned.1.call-update) | async-done | bytes 884752
  503.0 29.7 %reduce-scatter.13.cloned.1.call-done = bf16[192,768]{1,0:T(8,128)(2,1)} async-done(((bf16[768,768]{1,0:T(8,128)(2,1)}), bf16[192,768]{1,0:T(8,128)(2,1)}) %reduce-scatter.13.cloned.1.call-update) | async-done | bytes 294928 | tf_op jit(solution)/shard_map/reduce_scatter | solution.py:212
  532.8 60.0 %reduce-scatter.15.cloned.1.call-done = bf16[192,3072]{1,0:T(8,128)(2,1)} async-done(((bf16[768,3072]{1,0:T(8,128)(2,1)}), bf16[192,3072]{1,0:T(8,128)(2,1)}) %reduce-scatter.15.cloned.1.call-update) | async-done | bytes 1179664 | tf_op jit(solution)/shard_map/reduce_scatter | solution.py:224
  592.8 59.8 %reduce-scatter.17.cloned.1.call-done = bf16[768,768]{1,0:T(8,128)(2,1)} async-done(((bf16[3072,768]{1,0:T(8,128)(2,1)}), bf16[768,768]{1,0:T(8,128)(2,1)}) %reduce-scatter.17.cloned.1.call-update) | async-done | bytes 1179664 | tf_op jit(solution)/shard_map/reduce_scatter | solution.py:230
  659.2 16.7 %all-reduce.19 = (bf16[768]{0:T(1024)(128)(2,1)}, bf16[768]{0:T(1024)(128)(2,1)}, bf16[768]{0:T(1024)(128)(2,1)}, bf16[768]{0:T(1024)(128)(2,1)}, bf16[768]{0:T(...) all-reduce(bf16[768]{0:T(1024)(128)(2,1)} %dynamic-update-slice.7, ...), channel_id=1, replica_groups=mesh['shard'=4,'ctx'=8] {'shard'}, use_global_device_ids=true, to_apply=%add.7 | all-reduce | flops 9984 | bytes 39936
  686.7 15.6 %all-reduce.17 = (bf16[192]{0:T(256)(128)(2,1)}, bf16[192]{0:T(256)(128)(2,1)}, bf16[192]{0:T(256)(128)(2,1)}, bf16[192]{0:T(256)(128)(2,1)}, bf16[192]{0:T(256)...) all-reduce(bf16[192]{0:T(256)(128)(2,1)} %dynamic-slice.9, ...), channel_id=1, replica_groups=mesh['shard'=4,'ctx'=8] {'ctx'}, use_global_device_ids=true, to_apply=%region_21.22 | all-reduce | flops 2304 | bytes 9216 | tf_op jit(solution)/shard_map/psum | solution.py:245
  718.3 28.3 %all-reduce.23.cloned.1.call-done = (bf16[192,2304]{0,1:T(8,128)(2,1)}, bf16[192,768]{1,0:T(8,128)(2,1)}, bf16[192,3072]{1,0:T(8,128)(2,1)}, bf16[768,768]{1,0:T(8,128)(2,1)}) async-done(((bf16[192,2304]{0,1:T(8,128)(2,1)}, bf16[192,768]{1,0:T(8,128)(2,1)}, bf16[192,3072]{1,0:T(8,128)(2,1)}, bf16[768,768]{1,0:T(8,128)(2,1)}), (bf16[192,2304]{0,1:T(8,128)(2,1)}, bf16[192,768]{1,0:T(8,128)(2,1)}, ...) | async-done | bytes 3538960 | tf_op jit(solution)/shard_map/psum | solution.py:244
  (325 shorter events, 226.3 us)
Async XLA Ops:
  7.2 52.7 %all-gather.8.cloned.1.call-start = ((), (), s32[]{:S(2)}) async-start(), calls=%async_computation.6 | async-start | bytes 4423680 | tf_op jit(solution)/shard_map/all_gather | solution.py:63
  7.9 83.3 %all-gather.10.cloned.1.call-start = ((), (), s32[]{:S(2)}) async-start(), calls=%async_computation.7 | async-start | bytes 1769472 | tf_op jit(solution)/shard_map/all_gather | solution.py:104
  63.9 55.3 %all-gather.12.cloned.1.call-start = ((), (), s32[]{:S(2)}) async-start(), calls=%async_computation.8 | async-start | bytes 1769472 | tf_op jit(solution)/shard_map/all_gather | solution.py:103
  64.7 110.5 %all-gather.14.cloned.1.call-start = ((), (), s32[]{:S(2)}) async-start(), calls=%async_computation.9 | async-start | bytes 1474560 | tf_op jit(solution)/shard_map/all_gather | solution.py:66
  65.3 140.8 %all-gather.16.cloned.1.call-start = ((), (), s32[]{:S(2)}) async-start(), calls=%async_computation.10 | async-start | bytes 5898240 | tf_op jit(solution)/shard_map/all_gather | solution.py:70
  65.9 198.8 %all-gather.18.cloned.1.call-start = ((), (), s32[]{:S(2)}) async-start(), calls=%async_computation.11 | async-start | bytes 5898240 | tf_op jit(solution)/shard_map/all_gather | solution.py:72
  66.5 343.5 %reduce-scatter.19.cloned.1.call-start = ((), (), s32[]{:S(2)}) async-start(), calls=%async_computation.15 | async-start | bytes 1769472
  119.3 55.9 %copy-start.5 = (bf16[1,128,768]{2,1,0:T(8,128)(2,1)S(1)}, bf16[1,128,768]{2,1,0:T(8,128)(2,1)}, u32[]{:S(2)}) copy-start(bf16[1,128,768]{2,1,0:T(8,128)(2,1)} %param.20) | copy-start | bytes 589828
  175.2 38.5 %copy-start.9 = (bf16[12,64,128]{2,1,0:T(8,128)(2,1)}, bf16[12,64,128]{2,1,0:T(8,128)(2,1)S(1)}, u32[]{:S(2)}) copy-start(bf16[12,64,128]{2,1,0:T(8,128)(2,1)S(1)} %convert_element_type.205) | copy-start | bytes 589828
  177.2 98.2 %copy-start.16 = (f32[128]{0:T(128)}, f32[128]{0:T(128)S(1)}, u32[]{:S(2)}) copy-start(f32[128]{0:T(128)S(1)} %add_rsqrt_fusion.1) | copy-start | bytes 1540
  268.1 7.3 copy-start.18
  268.3 7.1 copy-start.21
  279.3 175.9 %copy-start.2 = (f32[128,768]{1,0:T(8,128)}, f32[128,768]{1,0:T(8,128)S(1)}, u32[]{:S(2)}) copy-start(f32[128,768]{1,0:T(8,128)S(1)} %get-tuple-element.291) | copy-start | bytes 1179652
  375.6 69.7 %reduce-scatter.21.cloned.1.call-start = ((), (), s32[]{:S(2)}) async-start(), calls=%async_computation.16 | async-start | bytes 1769472
  378.3 122.4 %reduce-scatter.23.cloned.1.call-start = ((), (), s32[]{:S(2)}) async-start(), calls=%async_computation.17 | async-start | bytes 4423680
  379.3 70.0 %copy-start.8 = (bf16[12,64,128]{2,1,0:T(8,128)(2,1)}, bf16[12,64,128]{2,1,0:T(8,128)(2,1)S(1)}, u32[]{:S(2)}) copy-start(bf16[12,64,128]{2,1,0:T(8,128)(2,1)S(1)} %get-tuple-element.298) | copy-start | bytes 589828
  411.0 38.3 %copy-start.6 = (bf16[768,128]{1,0:T(8,128)(2,1)}, bf16[768,128]{1,0:T(8,128)(2,1)S(1)}, u32[]{:S(2)}) copy-start(bf16[768,128]{1,0:T(8,128)(2,1)S(1)} %copy.41) | copy-start | bytes 589828
  455.1 77.6 %reduce-scatter.13.cloned.1.call-start = ((), (), s32[]{:S(2)}) async-start(), calls=%async_computation.12 | async-start | bytes 1474560 | tf_op jit(solution)/shard_map/reduce_scatter | solution.py:212
  457.5 135.3 %reduce-scatter.15.cloned.1.call-start = ((), (), s32[]{:S(2)}) async-start(), calls=%async_computation.13 | async-start | bytes 5898240 | tf_op jit(solution)/shard_map/reduce_scatter | solution.py:224
  461.3 191.4 %reduce-scatter.17.cloned.1.call-start = ((), (), s32[]{:S(2)}) async-start(), calls=%async_computation.14 | async-start | bytes 5898240 | tf_op jit(solution)/shard_map/reduce_scatter | solution.py:230
  464.9 281.7 %all-reduce.23.cloned.1.call-start = ((), (), s32[]{:S(2)}) async-start(), calls=%async_computation.18 | async-start | bytes 7667712 | tf_op jit(solution)/shard_map/psum | solution.py:244
  652.6 6.6 copy-start.20
  652.6 60.5 %copy-start.19 = (f32[128]{0:T(128)S(1)}, f32[128]{0:T(128)}, u32[]{:S(2)}) copy-start(f32[128]{0:T(128)} %copy-done.18) | copy-start | bytes 1540
  652.6 62.3 %copy-start = (bf16[768,2304]{1,0:T(8,128)(2,1)S(1)}, bf16[768,2304]{1,0:T(8,128)(2,1)}, u32[]{:S(2)}) copy-start(bf16[768,2304]{1,0:T(8,128)(2,1)} %all-gather.8.cloned.1.call-done) | copy-start | bytes 10616836
  (15 other events, 45.1 us)
Sparse Core Ops, SparseCore 0:
  9.8 49.9 all-gather.7
  64.0 27.0 all-gather.9
  93.3 25.8 all-gather.11
  121.0 26.3 all-gather.13
  149.1 56.9 all-gather.15
  207.7 56.9 all-gather.17
  375.7 34.1 reduce-scatter.18
  412.8 32.5 reduce-scatter.20
  455.2 45.4 reduce-scatter.22
  504.1 28.6 reduce-scatter.12
  535.8 56.9 reduce-scatter.14
  595.6 56.9 reduce-scatter.16
  655.8 90.7 all-reduce.22
where the time goes:
time: 764 us; the launch traced here: 760 us
  waiting for transfers between devices  431 us (56%)
  matrix products  140 us (18%)
  local copies, waits for them, and re-layouts  66.7 us (9%)
  blocking collectives  58.9 us (8%)
  other arithmetic  46.2 us (6%)
  between operations  16.2 us (2%)
    dot_general x94, matrix products, contract_dims(): lax.dot_general(left, right, (((left_dim,), (right_dim,)), ((), ())), pre...  129 us
    unnamed x16, waiting for transfers between devices  103 us
    reduce_scatter x1, waiting for transfers between devices, local(): lax.psum_scatter(grads[7].astype(jnp.bfloat16), 'shard', scatter_dimensio...  60 us
    reduce_scatter x1, waiting for transfers between devices, local(): lax.psum_scatter(grads[9].astype(jnp.bfloat16), 'shard', scatter_dimensio...  59.8 us
    all_gather x1, waiting for transfers between devices, local(): lax.all_gather(w_down, 'shard', axis=0, tiled=True)  51 us
    unnamed x86, local copies, waits for them, and re-layouts  37.9 us
    unnamed x2, blocking collectives  35 us
    reduce_scatter x1, waiting for transfers between devices, local(): lax.psum_scatter(grads[3].astype(jnp.bfloat16), 'shard', scatter_dimensio...  29.7 us
  transfers between devices with their start and end apart: 13, of which 12 were waited for; matrix products, arithmetic and copies ran while one was open for 16% of the time, Pallas kernels for 0%

commit v1 on v0

v1 whole, which is shorter than its diff:
```python
import functools
import math

import jax
import jax.numpy as jnp
from jax import lax
from jax.experimental import pallas as pl
from jax.experimental.pallas import tpu as pltpu
from jax.sharding import PartitionSpec as P

HEADS = 12
EPS = 1e-06
MESH = pl.DeviceIdType.MESH
F32 = jnp.float32
BF16 = jnp.bfloat16
VMEM_LIMIT = 60 * 1024 * 1024


def normalize(z):
    centre = z - jnp.mean(z, axis=-1, keepdims=True)
    rstd = lax.rsqrt(jnp.mean(centre * centre, axis=-1, keepdims=True) + EPS)
    return (centre * rstd, rstd)


def norm_back(dnorm, normed, rstd):
    return rstd * (
        dnorm
        - jnp.mean(dnorm, axis=-1, keepdims=True)
        - normed * jnp.mean(dnorm * normed, axis=-1, keepdims=True)
    )


def gelu_exact(t):
    return jax.nn.gelu(t, approximate=False)


def contract_dims(left, right, left_dim, right_dim):
    return lax.dot_general(
        left, right, (((left_dim,), (right_dim,)), ((), ())), preferred_element_type=F32
    )


class Place:
    def __init__(self, n):
        self.n = n
        self.s = lax.axis_index("shard")
        self.c = lax.axis_index("ctx")
        self.core = lax.rem(self.c, 2)
        self.m = lax.div(self.c, 2)
        self.sib = self.m * 2 + (1 - self.core)
        self.p = self.flip(self.s)
        self.right = self.at(1)
        self.left = self.at(-1)

    def flip(self, q):
        half = self.n // 2
        return jnp.where(q < half, q, 3 * half - 1 - q)

    def at(self, offset):
        return self.flip(lax.rem(self.p + (offset % self.n), self.n))


def greet(peers):
    barrier = pltpu.get_barrier_semaphore()
    for peer in peers:
        pl.semaphore_signal(barrier, inc=1, device_id=peer, device_id_type=MESH)
    pl.semaphore_wait(barrier, len(peers))


def remote(src, dst, send, recv, peer):
    return pltpu.make_async_remote_copy(
        src_ref=src, dst_ref=dst, send_sem=send, recv_sem=recv, device_id=peer, device_id_type=MESH
    )


def gather_kernel(n, pairs, nw, small, kv, *refs):
    total = nw + int(small) + int(kv)
    ins, outs, sems = refs[:total], refs[total : 2 * total], refs[2 * total :]
    send, recv, dsend, drecv, lsem, ssend, srecv, ksend, krecv, esend, erecv = sems
    here = Place(n)
    s, c, m, core = here.s, here.c, here.m, here.core
    across = [(s, lax.rem(m + k, pairs) * 2 + core) for k in range(1, pairs)] if kv else []
    greet([(here.right, c), (here.left, c), (s, here.sib)] + across)

    def key(i, d, t):
        return (i * 2 + d) * (n - 1) + t

    def part(i, d, block=None):
        rows, cols = ins[i].shape
        where = (pl.ds(pl.multiple_of(core * (rows // 2), rows // 2), rows // 2),
                 pl.ds(d * (cols // 2), cols // 2))
        return ins[i].at[where] if block is None else outs[i].at[(block,) + where]

    def ring(i, d, t):
        owner = here.at(-t if d == 0 else t)
        k = key(i, d, t)
        return remote(
            part(i, d) if t == 0 else part(i, d, owner),
            part(i, d, owner),
            send.at[k], recv.at[k],
            (here.right if d == 0 else here.left, c),
        )

    def pair(i, d, t):
        owner = here.at(-1 - t if d == 0 else 1 + t)
        k = key(i, d, t)
        return remote(part(i, d, owner), part(i, d, owner), dsend.at[k], drecv.at[k], (s, here.sib))

    def small_ring(t):
        owner = here.at(-t)
        return remote(
            ins[nw] if t == 0 else outs[nw].at[owner],
            outs[nw].at[owner],
            ssend.at[t], srecv.at[t],
            (here.right, c),
        )

    kin, kout = ins[-1], outs[-1]

    def kv_send(k):
        return remote(kin, kout.at[c], ksend.at[k - 1], krecv.at[k - 1], across[k - 1])

    def kv_pair(k):
        block = lax.rem(m + pairs - k, pairs) * 2 + core
        return remote(
            kin if k == 0 else kout.at[block], kout.at[block], esend.at[k], erecv.at[k], (s, here.sib)
        )

    local = [
        pltpu.make_async_copy(ins[i], outs[i].at[c if kv and i == total - 1 else s], lsem.at[i])
        for i in range(total)
    ]
    if kv:
        for k in range(1, pairs):
            kv_send(k).start()
        kv_pair(0).start()
    if small:
        small_ring(0).start()
    for i in range(nw):
        for d in range(2):
            ring(i, d, 0).start()
    for copy in local:
        copy.start()
    for t in range(n - 1):
        if small:
            small_ring(t).wait_recv()
            if t + 1 < n - 1:
                small_ring(t + 1).start()
        for i in range(nw):
            for d in range(2):
                ring(i, d, t).wait_recv()
                if t + 1 < n - 1:
                    ring(i, d, t + 1).start()
                pair(i, d, t).start()
    if kv:
        for k in range(1, pairs):
            kv_send(k).wait_recv()
            kv_pair(k).start()
    for copy in local:
        copy.wait()
    for t in range(n - 1):
        if small:
            small_ring(t).wait_send()
        for i in range(nw):
            for d in range(2):
                ring(i, d, t).wait_send()
                pair(i, d, t).wait()
    if kv:
        for k in range(1, pairs):
            kv_send(k).wait_send()
        for k in range(pairs):
            kv_pair(k).wait()


def gather(n, pairs, cid, weights, small=None, kv=None):
    nw = len(weights)
    args = list(weights)
    shapes = [jax.ShapeDtypeStruct((n,) + w.shape, w.dtype) for w in weights]
    if small is not None:
        args.append(small)
        shapes.append(jax.ShapeDtypeStruct((n,) + small.shape, small.dtype))
    if kv is not None:
        args.append(kv)
        shapes.append(jax.ShapeDtypeStruct((2 * pairs,) + kv.shape, kv.dtype))
    dma = pltpu.SemaphoreType.DMA
    count = nw * 2 * (n - 1)
    outs = pl.pallas_call(
        functools.partial(gather_kernel, n, pairs, nw, small is not None, kv is not None),
        out_shape=shapes,
        in_specs=[pl.BlockSpec(memory_space=pltpu.VMEM)] * len(args),
        out_specs=[pl.BlockSpec(memory_space=pl.ANY)] * len(args),
        scratch_shapes=[dma((count,))] * 4
        + [dma((len(args),))]
        + [dma((n - 1,))] * 2
        + [dma((pairs,))] * 4,
        compiler_params=pltpu.CompilerParams(
            collective_id=cid, has_side_effects=True, vmem_limit_bytes=VMEM_LIMIT
        ),
        name=f"gather{cid}",
    )(*args)
    return list(outs)


def add_into(dst, sources, rows, cols, chunk=16):
    def view(item, r):
        ref, lead, row0, col0 = item
        start = pl.multiple_of(row0 + r * chunk, chunk)
        return ref.at[lead + (pl.ds(start, chunk), pl.ds(col0, cols))]

    def step(r, carry):
        value = view(sources[0], r)[...].astype(F32)
        for item in sources[1:]:
            value = value + view(item, r)[...].astype(F32)
        out = view(dst, r)
        out[...] = value.astype(out.dtype)
        return carry

    lax.fori_loop(0, rows // chunk, step, 0)


def scatter_kernel(n, pairs, nw, units, kv, *refs):
    nin = nw + int(kv)
    ins, outs = refs[:nin], refs[nin : 2 * nin]
    rest = refs[2 * nin :]
    got, acc, hop, up, down = (rest[j * nw : (j + 1) * nw] for j in range(5))
    rest = rest[5 * nw :]
    if kv:
        mate, far = rest[:2]
        rest = rest[2:]
    gsend, grecv, rsend, rrecv, usend, urecv, vrecv, bsend, brecv, osend, orecv = rest[:11]
    here = Place(n)
    s, c, m, core = here.s, here.c, here.m, here.core
    sib = (s, here.sib)
    above = lax.rem(m + 1, pairs) * 2 + core
    below = lax.rem(m + pairs - 1, pairs) * 2 + core
    root = pairs // 2
    if kv:
        across = [(s, lax.rem(m + k, pairs) * 2 + core) for k in range(1, pairs)]
    else:
        across = [(s, above), (s, below)]
    greet([(here.right, c), (here.left, c), sib] + across)

    offsets = []
    for k in range(1, n // 2 + 1):
        for o in (-k, k):
            if o % n not in [q % n for q in offsets]:
                offsets.append(o)
    offsets.append(0)

    def half_rows(i):
        return ins[i].shape[1] // 2

    def mine(i):
        return pl.multiple_of(core * half_rows(i), half_rows(i))

    def theirs(i):
        return pl.multiple_of((1 - core) * half_rows(i), half_rows(i))

    def swap(i, j):
        block = here.at(offsets[j])
        k = i * n + j
        return remote(
            ins[i].at[block, pl.ds(theirs(i), half_rows(i)), :],
            got[i].at[block],
            gsend.at[k], grecv.at[k], sib,
        )

    if kv:
        din, dout = ins[-1], outs[-1]
        ksend, krecv, esend, erecv = rest[11:15]
        token_rows, token_cols = din.shape[1:]

        def kv_swap(k):
            q = lax.rem(m + k, pairs)
            return remote(din.at[q * 2 + 1 - core], mate.at[q], esend.at[k], erecv.at[k], sib)

        def kv_send(k):
            q = lax.rem(m + k, pairs)
            return remote(
                mate.at[q], far.at[k - 1], ksend.at[k - 1], krecv.at[k - 1], across[k - 1]
            )

        for k in list(range(1, pairs)) + [0]:
            kv_swap(k).start()
    for j in range(n):
        for i in range(nw):
            swap(i, j).start()
    if kv:
        for k in list(range(1, pairs)) + [0]:
            q = lax.rem(m + k, pairs)
            kv_swap(k).wait_recv()
            add_into((mate, (q,), 0, 0), [(mate, (q,), 0, 0), (din, (q * 2 + core,), 0, 0)],
                     token_rows, token_cols)
            if k:
                kv_send(k).start()
    for j in range(n):
        block = here.at(offsets[j])
        for i in range(nw):
            swap(i, j).wait_recv()
            add_into((acc[i], (block,), 0, 0),
                     [(got[i], (block,), 0, 0), (ins[i], (block,), mine(i), 0)],
                     half_rows(i), ins[i].shape[2])

    def region(k, d):
        i, piece, width = units[k]
        return i, half_rows(i), d * (ins[i].shape[2] // 2) + piece * width, width

    def ring(k, d, t):
        i, rows, col, width = region(k, d)
        block = here.at(-1 - t if d == 0 else 1 + t)
        q = (k * 2 + d) * (n - 1) + t
        return remote(
            acc[i].at[block, :, pl.ds(col, width)],
            hop[i].at[t, :, pl.ds(col, width)],
            rsend.at[q], rrecv.at[q],
            (here.right if d == 0 else here.left, c),
        )

    def own(k, d):
        i, rows, col, width = region(k, d)
        return acc[i].at[s, :, pl.ds(col, width)]

    def climb(k, d):
        i, rows, col, width = region(k, d)
        q = k * 2 + d
        return remote(own(k, d), up[i].at[:, pl.ds(col, width)], usend.at[q], urecv.at[q], (s, above))

    def descend(k, d):
        i, rows, col, width = region(k, d)
        q = k * 2 + d
        return remote(own(k, d), down[i].at[:, pl.ds(col, width)], usend.at[q], vrecv.at[q], (s, below))

    def final(k, d):
        i, rows, col, width = region(k, d)
        return outs[i].at[pl.ds(mine(i), rows), pl.ds(col, width)]

    def share(k, d, side):
        q = k * 2 + d
        return remote(
            final(k, d), final(k, d), bsend.at[q * 2 + side], brecv.at[q], (s, above if side else below)
        )

    def twin(k, d):
        q = k * 2 + d
        return remote(final(k, d), final(k, d), osend.at[q], orecv.at[q], sib)

    def ring_step(t, k, d):
        i, rows, col, width = region(k, d)
        if t >= 0:
            ring(k, d, t).wait_recv()
            block = here.at(-2 - t if d == 0 else 2 + t)
            add_into((acc[i], (block,), 0, col), [(acc[i], (block,), 0, col), (hop[i], (t,), 0, col)],
                     rows, width)
        if t + 1 < n - 1:
            ring(k, d, t + 1).start()

    def chain_step(h, k, d):
        i, rows, col, width = region(k, d)

        @pl.when((m == h) & (m < root))
        def _():
            if h > 0:
                climb(k, d).wait_recv()
                add_into((acc[i], (s,), 0, col), [(acc[i], (s,), 0, col), (up[i], (), 0, col)],
                         rows, width)
            climb(k, d).start()

        @pl.when((m == pairs - 1 - h) & (m > root))
        def _():
            if h > 0:
                descend(k, d).wait_recv()
                add_into((acc[i], (s,), 0, col), [(acc[i], (s,), 0, col), (down[i], (), 0, col)],
                         rows, width)
            descend(k, d).start()

    def root_step(k, d):
        i, rows, col, width = region(k, d)

        @pl.when(m == root)
        def _():
            items = [(acc[i], (s,), 0, col)]
            if root > 0:
                climb(k, d).wait_recv()
                items.append((up[i], (), 0, col))
            if root < pairs - 1:
                descend(k, d).wait_recv()
                items.append((down[i], (), 0, col))
            add_into((outs[i], (), mine(i), col), items, rows, width)
            if root > 0:
                share(k, d, 0).start()
            if root < pairs - 1:
                share(k, d, 1).start()
            twin(k, d).start()

    def back_step(h, k, d):
        @pl.when(m == root - h)
        def _():
            share(k, d, 0).wait_recv()
            if root - h > 0:
                share(k, d, 0).start()
            twin(k, d).start()

        @pl.when(m == root + h)
        def _():
            share(k, d, 1).wait_recv()
            if root + h < pairs - 1:
                share(k, d, 1).start()
            twin(k, d).start()

    stages = [functools.partial(ring_step, t) for t in range(-1, n - 1)]
    stages += [functools.partial(chain_step, h) for h in range(max(root, pairs - 1 - root))]
    stages += [root_step]
    stages += [functools.partial(back_step, h) for h in range(1, max(root, pairs - 1 - root) + 1)]
    for tick in range(len(units) + len(stages) - 1):
        for stage in reversed(range(len(stages))):
            k = tick - stage
            if 0 <= k < len(units):
                for d in range(2):
                    stages[stage](k, d)

    if kv:
        items = [(mate, (m,), 0, 0)]
        for k in range(1, pairs):
            kv_send(k).wait_recv()
            items.append((far, (k - 1,), 0, 0))
        add_into((dout, (), 0, 0), items, token_rows, token_cols)
        for k in range(pairs):
            kv_swap(k).wait_send()
            if k:
                kv_send(k).wait_send()
    for i in range(nw):
        for j in range(n):
            swap(i, j).wait_send()
    for k in range(len(units)):
        for d in range(2):
            for t in range(n - 1):
                ring(k, d, t).wait_send()

            @pl.when(m != root)
            def _():
                climb(k, d).wait_send()

            @pl.when((m > 0) & (m <= root))
            def _():
                share(k, d, 0).wait_send()

            @pl.when((m >= root) & (m < pairs - 1))
            def _():
                share(k, d, 1).wait_send()

            twin(k, d).wait()


def scatter(n, pairs, cid, grads, kv=None):
    nw = len(grads)
    units = []
    for i, g in enumerate(grads):
        width = g.shape[2] // 2
        pieces = 3 if width % 384 == 0 and width * g.shape[1] >= 200000 else 1
        units += [(i, j, width // pieces) for j in range(pieces)]
    args = list(grads)
    shapes = [jax.ShapeDtypeStruct(g.shape[1:], BF16) for g in grads]
    vm = pltpu.VMEM
    halves = [(g.shape[1] // 2, g.shape[2]) for g in grads]
    scratch = [vm((n,) + h, BF16) for h in halves] * 2
    scratch += [vm((n - 1,) + h, BF16) for h in halves]
    scratch += [vm(h, BF16) for h in halves] * 2
    dma = pltpu.SemaphoreType.DMA
    both = 2 * len(units)
    sems = [dma((nw * n,))] * 2 + [dma((both * (n - 1),))] * 2 + [dma((both,))] * 3
    sems += [dma((2 * both,)), dma((both,)), dma((both,)), dma((both,))]
    if kv is not None:
        args.append(kv)
        shapes.append(jax.ShapeDtypeStruct(kv.shape[1:], F32))
        scratch += [vm((pairs,) + kv.shape[1:], BF16), vm((pairs - 1,) + kv.shape[1:], BF16)]
        sems += [dma((pairs,))] * 4
    outs = pl.pallas_call(
        functools.partial(scatter_kernel, n, pairs, nw, tuple(units), kv is not None),
        out_shape=shapes,
        in_specs=[pl.BlockSpec(memory_space=pltpu.VMEM)] * len(args),
        out_specs=[pl.BlockSpec(memory_space=pltpu.VMEM)] * len(args),
        scratch_shapes=scratch + sems,
        compiler_params=pltpu.CompilerParams(
            collective_id=cid, has_side_effects=True, vmem_limit_bytes=VMEM_LIMIT
        ),
        name=f"scatter{cid}",
    )(*args)
    return list(outs)


def lanes(ref):
    return jnp.concatenate([ref[j] for j in range(ref.shape[0])], axis=1)


def attend_kernel(scale, q_ref, k_ref, v_ref, valid_ref, ctx_ref, lse_ref):
    scores = contract_dims(q_ref[...], lanes(k_ref), 0, 0) * scale
    scores = jnp.where(valid_ref[...] > 0, scores, -1e30)
    peak = jnp.max(scores, axis=1, keepdims=True)
    weight = jnp.exp(scores - peak)
    norm = jnp.sum(weight, axis=1, keepdims=True)
    lse_ref[0] = peak + jnp.log(norm)
    probs = (weight * (1.0 / norm)).astype(BF16)
    ctx_ref[...] = contract_dims(lanes(v_ref), probs, 1, 1)


def attend(scale, query_t, kv, valid):
    width, toks = query_t.shape
    size = width // HEADS
    blocks = kv.shape[0]
    return pl.pallas_call(
        functools.partial(attend_kernel, scale),
        grid=(HEADS,),
        out_shape=(
            jax.ShapeDtypeStruct((width, toks), F32),
            jax.ShapeDtypeStruct((HEADS, toks, 1), F32),
        ),
        in_specs=[
            pl.BlockSpec((size, toks), lambda h: (h, 0)),
            pl.BlockSpec((blocks, size, toks), lambda h: (0, h, 0)),
            pl.BlockSpec((blocks, size, toks), lambda h: (0, HEADS + h, 0)),
            pl.BlockSpec(valid.shape, lambda h: (0, 0)),
        ],
        out_specs=(
            pl.BlockSpec((size, toks), lambda h: (h, 0)),
            pl.BlockSpec((1, toks, 1), lambda h: (h, 0, 0)),
        ),
        compiler_params=pltpu.CompilerParams(vmem_limit_bytes=VMEM_LIMIT // 2),
        name="attend",
    )(query_t, kv, kv, valid)


def attend_back_kernel(
    scale, q_ref, k_ref, v_ref, valid_ref, lse_ref, dctx_ref, ctx_ref, dq_ref, dk_ref, dv_ref
):
    query, keys, values = q_ref[...], lanes(k_ref), lanes(v_ref)
    dctx = dctx_ref[...]
    dctx_b = dctx.astype(BF16)
    delta_row = jnp.sum(dctx * ctx_ref[...], axis=0, keepdims=True)
    delta = jnp.transpose(jnp.broadcast_to(delta_row, (8, delta_row.shape[1])))[:, :1]
    scores = contract_dims(query, keys, 0, 0) * scale
    scores = jnp.where(valid_ref[...] > 0, scores, -1e30)
    prob = jnp.exp(scores - lse_ref[0])
    dvalue = jnp.dot(dctx_b, prob.astype(BF16), preferred_element_type=F32)
    dprob = contract_dims(dctx_b, values, 0, 0)
    dscore = (prob * (dprob - delta)).astype(BF16)
    dq_ref[...] = contract_dims(keys, dscore, 1, 1) * scale
    dkey = jnp.dot(query, dscore, preferred_element_type=F32) * scale
    toks = query.shape[1]
    for j in range(dk_ref.shape[0]):
        dk_ref[j] = dkey[:, j * toks : (j + 1) * toks].astype(BF16)
        dv_ref[j] = dvalue[:, j * toks : (j + 1) * toks].astype(BF16)


def attend_back(scale, query_t, kv, valid, lse, dctx_t, ctx_t):
    width, toks = query_t.shape
    size = width // HEADS
    blocks = kv.shape[0]
    head = pl.BlockSpec((size, toks), lambda h: (h, 0))
    keys = pl.BlockSpec((blocks, size, toks), lambda h: (0, h, 0))
    return pl.pallas_call(
        functools.partial(attend_back_kernel, scale),
        grid=(HEADS,),
        out_shape=(
            jax.ShapeDtypeStruct((width, toks), F32),
            jax.ShapeDtypeStruct((blocks, width, toks), BF16),
            jax.ShapeDtypeStruct((blocks, width, toks), BF16),
        ),
        in_specs=[
            head,
            keys,
            pl.BlockSpec((blocks, size, toks), lambda h: (0, HEADS + h, 0)),
            pl.BlockSpec(valid.shape, lambda h: (0, 0)),
            pl.BlockSpec((1, toks, 1), lambda h: (h, 0, 0)),
            head,
            head,
        ],
        out_specs=(head, keys, keys),
        compiler_params=pltpu.CompilerParams(vmem_limit_bytes=VMEM_LIMIT // 2),
        name="attend_back",
    )(query_t, kv, kv, valid, lse, dctx_t, ctx_t)


def local(
    n,
    n_ctx,
    tokens,
    lengths,
    cotangent,
    w_qkv,
    b_query,
    b_value,
    w_out,
    b_out,
    ln1_gain,
    ln1_bias,
    w_up,
    b_up,
    w_down,
    b_down,
    ln2_gain,
    ln2_bias,
):
    pairs = n_ctx // 2
    x = tokens[0]
    toks, width = x.shape
    scale = 1.0 / math.sqrt(width // HEADS)
    limit = lengths[0]
    vectors = (b_query, b_value, b_out, ln1_gain, ln1_bias, b_down, ln2_gain, ln2_bias, b_up)
    lens = [v.shape[0] for v in vectors]
    flat = jnp.concatenate(vectors)
    lane = 256
    rows = -(-sum(lens) // lane)
    rows = -(-rows // 32) * 32
    flat = jnp.pad(flat, (0, rows * lane - sum(lens))).reshape(rows, lane)
    wq_all, small_all = gather(n, pairs, 0, [w_qkv], small=flat)
    wq_full = wq_all.reshape(width, -1)
    small_all = small_all.reshape(n, rows * lane)
    parts, at = [], 0
    for size in lens:
        parts.append(small_all[:, at : at + size].reshape(-1).astype(F32))
        at += size
    bq, bv, bo, g1, c1, bd, g2, c2, bu = parts

    qkv_t = contract_dims(wq_full, x, 0, 1)
    query_t = (qkv_t[:width] + bq[:, None]).astype(BF16)
    shift = jnp.concatenate([jnp.zeros((width,), F32), bv])
    kv_t = (qkv_t[width:] + shift[:, None]).astype(BF16)
    wo_all, wu_all, wd_all, kv = gather(n, pairs, 1, [w_out, w_up, w_down], kv=kv_t)
    wo_full = wo_all.reshape(width, -1)
    wu_full = wu_all.reshape(width, -1)
    wd_full = wd_all.reshape(-1, width)
    valid = (jnp.arange(n_ctx * toks, dtype=jnp.int32) < limit).astype(F32)[None, :]

    ctx_t, lse = attend(scale, query_t, kv, valid)
    context_b_t = ctx_t.astype(BF16)
    z_one = x.astype(F32) + contract_dims(context_b_t, wo_full, 0, 0) + bo
    n_one, rstd_one = normalize(z_one)
    x_one = n_one * g1 + c1
    x_one_b = x_one.astype(BF16)
    upper = jnp.dot(x_one_b, wu_full, preferred_element_type=F32) + bu
    hidden_f, gelu_back = jax.vjp(gelu_exact, upper)
    hidden = hidden_f.astype(BF16)
    z_two = x_one + jnp.dot(hidden, wd_full, preferred_element_type=F32) + bd
    n_two, rstd_two = normalize(z_two)
    out = (n_two * g2 + c2).astype(BF16)
    grad = cotangent[0].astype(F32)
    dg_two = jnp.sum(grad * n_two, axis=0)
    db_two = jnp.sum(grad, axis=0)
    dz_two = norm_back(grad * g2, n_two, rstd_two)
    dz_two_b = dz_two.astype(BF16)
    dw_down = contract_dims(hidden, dz_two_b, 0, 0)
    db_down = jnp.sum(dz_two, axis=0)
    dhid = contract_dims(dz_two_b, wd_full, 1, 1)
    dupper = gelu_back(dhid)[0]
    dupper_b = dupper.astype(BF16)
    dw_up = contract_dims(x_one_b, dupper_b, 0, 0)
    db_up = jnp.sum(dupper, axis=0)
    dx_one = dz_two + contract_dims(dupper_b, wu_full, 1, 1)
    dg_one = jnp.sum(dx_one * n_one, axis=0)
    db_one = jnp.sum(dx_one, axis=0)
    dz_one = norm_back(dx_one * g1, n_one, rstd_one)
    dz_one_b = dz_one.astype(BF16)
    dw_out = contract_dims(context_b_t, dz_one_b, 1, 0)
    db_out = jnp.sum(dz_one, axis=0)
    dctx_t = contract_dims(wo_full, dz_one_b, 1, 1)

    query_grad_t, dkeys, dvalues = attend_back(scale, query_t, kv, valid, lse, dctx_t, ctx_t)
    dkv = jnp.concatenate([dkeys, dvalues], axis=1)

    def blocks(g):
        return g.astype(BF16).reshape(n, -1, g.shape[1])

    up_sum, down_sum, out_sum, kv_grad_t = scatter(
        n, pairs, 2, [blocks(dw_up), blocks(dw_down), blocks(dw_out)], kv=dkv
    )
    dqkv_b_t = jnp.concatenate([query_grad_t.astype(BF16), kv_grad_t.astype(BF16)], axis=0)
    dw_qkv = contract_dims(x, dqkv_b_t, 0, 1)
    dx = dz_one + contract_dims(dqkv_b_t, wq_full, 0, 1)
    db_query = jnp.sum(query_grad_t, axis=1)
    db_value = jnp.sum(kv_grad_t[width:], axis=1)
    small_grads = (db_query, db_value, db_out, dg_one, db_one, db_down, dg_two, db_two, db_up)
    packed = jnp.concatenate([g.astype(BF16).reshape(n, -1) for g in small_grads], axis=1)
    packed = jnp.pad(packed, ((0, 0), (0, rows * lane - packed.shape[1]))).reshape(n, rows, lane)
    qkv_sum, small_sum = scatter(n, pairs, 3, [blocks(dw_qkv), packed])
    small_sum = small_sum.reshape(rows * lane).astype(F32)
    pieces, at = [], 0
    for size in lens:
        pieces.append(small_sum[at : at + size])
        at += size
    gq, gv, go, gg1, gc1, gd, gg2, gc2, gu = pieces
    return (
        out[None],
        dx[None],
        qkv_sum.astype(F32),
        gq,
        gv,
        out_sum.astype(F32),
        go,
        gg1,
        gc1,
        up_sum.astype(F32),
        gu,
        down_sum.astype(F32),
        gd,
        gg2,
        gc2,
    )


def solution(mesh):
    rows, blocks, flat = P("shard", None), P("shard", "ctx", None), P("shard")
    in_specs = (
        blocks, flat, blocks, rows, flat, flat, rows, flat, flat, flat, rows, flat, rows, flat, flat, flat,
    )
    out_specs = (
        blocks, blocks, rows, flat, flat, rows, flat, flat, flat, rows, flat, rows, flat, flat, flat,
    )
    body = functools.partial(local, mesh.shape["shard"], mesh.shape["ctx"])
    return jax.shard_map(body, mesh=mesh, in_specs=in_specs, out_specs=out_specs, check_vma=False)
```

time: 764 us -> 313 us (0.41)
  waiting for transfers between devices: 431 us -> 0 us
  Pallas kernels: 0 us -> 242 us
  matrix products: 140 us -> 39.2 us
  blocking collectives: 58.9 us -> 0 us
  local copies, waits for them, and re-layouts: 66.7 us -> 14.7 us
  other arithmetic: 46.2 us -> 15.3 us
  between operations: 16.2 us -> 1.58 us
    pallas_call x0 -> x6, Pallas kernels: none -> 242 us  [the longest x2 144 us: scatter(): pl.pallas_call(functools.partial(scatter_kernel, n, pairs, nw, tuple(unit...]
    all_gather x6 -> x0, waiting for transfers between devices: 150 us -> none  [the longest x1 51 us: local(): lax.all_gather(w_down, 'shard', axis=0, tiled=True)]
    reduce_scatter x3 -> x0, waiting for transfers between devices: 150 us -> none  [the longest x1 60 us: local(): lax.psum_scatter(grads[7].astype(jnp.bfloat16), 'shard', scatter_dimensio...]
    unnamed x16 -> x0, waiting for transfers between devices: 103 us -> none
    dot_general x94 -> x10, matrix products: 129 us -> 28.3 us  [contract_dims(): lax.dot_general(left, right, (((left_dim,), (right_dim,)), ((), ())), pre...]
    unnamed x2 -> x0, blocking collectives: 35 us -> none
    unnamed x86 -> x53, local copies, waits for them, and re-layouts: 37.9 us -> 5.24 us
    psum x1 -> x0, waiting for transfers between devices: 28.3 us -> none  [local(): lax.psum(pieces[0].astype(jnp.bfloat16), 'ctx').astype(jnp.float32)]
  transfers between devices with their start and end apart: 13 -> 0, of which waited for: 12 -> 0; matrix products, arithmetic and copies ran while one was open for 16% -> 0% of each run, Pallas kernels for 0% -> 0%
where the time goes in v1:
time: 313 us
  Pallas kernels  242 us (77%)
  matrix products  39.2 us (13%)
  other arithmetic  15.3 us (5%)
  local copies, waits for them, and re-layouts  14.7 us (5%)
    pallas_call x2, Pallas kernels, scatter(): pl.pallas_call(functools.partial(scatter_kernel, n, pairs, nw, tuple(unit...  144 us
    pallas_call x2, Pallas kernels, gather(): pl.pallas_call(functools.partial(gather_kernel, n, pairs, nw, small is no...  79.6 us
    dot_general x10, matrix products, contract_dims(): lax.dot_general(left, right, (((left_dim,), (right_dim,)), ((), ())), pre...  28.3 us
    pallas_call x1, Pallas kernels, attend_back(): pl.pallas_call(functools.partial(attend_back_kernel, scale), grid=(HEADS,...  9.12 us
    pallas_call x1, Pallas kernels, attend(): pl.pallas_call(functools.partial(attend_kernel, scale), grid=(HEADS,), ou...  9.01 us
    dot_general x1, matrix products, local(): upper = jnp.dot(x_one_b, wu_full, preferred_element_type=F32) + bu  7.6 us

profile of v1, /device:TPU:0, one launch (start us, length us, event | category | flops | bytes accessed | tf_op | source)
XLA Modules:
  0.0 312.8 jit_solution(15001246021327890172)
XLA Ops:
  0.7 6.1 %concatenate.17 = bf16[2304]{0:T(1024)(128)(2,1)S(1)} concatenate(bf16[192]{0:T(256)(128)(2,1)} %param.20, bf16[192]{0:T(256)(128)(2,1)} %param.21, bf16[192]{0:T(256)(128)(2,1)} %param.23, bf16[192]{0:T(256)(128)(2,1)} %param.24, bf16[192]{0:T(256)(128)(2,1)} %param.25, bf16[192]{0:T(256)(128)(2,1)} %param.29, bf16[192]{0:T(256)(128)(2,1)} %param.30, bf16[192]{0:T(256)(128)(2,1)} %param.31, ...), dimensions={0} | concatenate | bytes 9216 | tf_op jit(solution)/shard_map/concatenate | solution.py:610
  7.4 25.0 %gather0.1 = (bf16[4,192,2304]{2,1,0:T(8,128)(2,1)}, bf16[4,32,256]{2,1,0:T(8,128)(2,1)}) custom-call(bf16[192,2304]{1,0:T(8,128)(2,1)} %refs_0_.2, bf16[32,256]{1,0:T(8,128)(2,1)} %reshape.213.refs_1_), custom_call_target="tpu_custom_call" | custom-call | tf_op jit(solution)/shard_map/gather0/pallas_call | solution.py:187
  34.0 3.1 fusion.23
  38.2 54.6 %gather1.1 = (bf16[4,192,768]{2,1,0:T(8,128)(2,1)}, bf16[4,192,3072]{2,1,0:T(8,128)(2,1)}, bf16[4,768,768]{2,1,0:T(8,128)(2,1)}, bf16[8,1536,128]{2,1,0:T(8,128)(2,1)}) custom-call(bf16[192,768]{1,0:T(8,128)(2,1)} %refs_0_.3, bf16[192,3072]{1,0:T(8,128)(2,1)} %refs_1_.1, bf16[768,768]{1,0:T(8,128)(2,1)} %refs_2_.1, bf16[1536,128]{1,0:T(8,128)(2,1)} %fusion.9.refs_3_), custom_call_target="tpu_custom_call" | custom-call | tf_op jit(solution)/shard_map/gather1/pallas_call | solution.py:187
  93.7 1.9 copy-done
  95.6 9.0 %attend.1 = (f32[768,128]{1,0:T(8,128)S(1)}, f32[12,128,1]{2,1,0:T(8,128)S(1)}) custom-call(bf16[768,128]{1,0:T(8,128)(2,1)S(1)} %fusion.17.q_ref, bf16[8,1536,128]{2,1,0:T(8,128)(2,1)S(1)} %copy-done, bf16[8,1536,128]{2,1,0:T(8,128)(2,1)S(1)} %copy-done, f32[1,1024]{1,0:T(1,128)S(1)} %compare_convert_fusion.valid_ref), custom_call_target="tpu_custom_call" | custom-call | tf_op jit(solution)/shard_map/attend/pallas_call | solution.py:510
  105.6 7.6 %multiply_convert_fusion = (bf16[128,3072]{1,0:T(8,128)(2,1)S(1)}, f32[128,3072]{1,0:T(8,128)}) fusion(f32[3072]{0:T(1024)S(1)} %reshape.229, bf16[768,3072]{1,0:T(8,128)(2,1)} %bitcast.55, f32[128,768]{1,0:T(8,128)S(1)} %get-tuple-element.80, f32[768]{0:T(1024)S(1)} %reshape.228, f32[768]{0:T(1024)S(1)} %reshape.227, f32[128]{0:T(128)S(1)} %add_rsqrt_fusion.1, ...), kind=kOutput, calls=%fused_computation.8 | convolution fusion | flops 630423552 | bytes 7490560 | tf_op jit(solution)/shard_map/dot_general | solution.py:640
  113.3 3.3 %fusion.45 = (f32[128]{0:T(128)S(1)}, f32[128,768]{1,0:T(8,128)S(1)}) fusion(f32[768]{0:T(1024)S(1)} %reshape.230, bf16[128,3072]{1,0:T(8,128)(2,1)S(1)} %get-tuple-element.81, bf16[3072,768]{1,0:T(8,128)(2,1)} %bitcast.59, f32[768]{0:T(1024)S(1)} %reshape.228, f32[768]{0:T(1024)S(1)} %reshape.227, f32[128]{0:T(128)S(1)} %add_rsqrt_fusion.1, ...), kind=kOutput, calls=%fused_computation.97 | convolution fusion | flops 604667776 | bytes 6302208 | tf_op jit(solution)/shard_map/dot_general | solution.py:643
  117.7 1.5 fusion.39
  119.1 8.1 %fusion.46 = (bf16[3072]{0:T(1024)(128)(2,1)}, bf16[128,3072]{1,0:T(8,128)(2,1)S(1)}) fusion(f32[128,3072]{1,0:T(8,128)} %get-tuple-element.82, bf16[3072,768]{1,0:T(8,128)(2,1)} %bitcast.60, f32[128,768]{1,0:T(8,128)S(1)} %get-tuple-element.57), kind=kOutput, calls=%fused_computation.98 | convolution fusion | flops 632779776 | bytes 7477248 | tf_op jit(solution)/shard_map/dot_general | solution.py:38
  127.2 2.4 multiply_reduce_fusion
  131.5 9.1 %attend_back.1 = (f32[768,128]{1,0:T(8,128)S(1)}, bf16[8,768,128]{2,1,0:T(8,128)(2,1)S(1)}, bf16[8,768,128]{2,1,0:T(8,128)(2,1)S(1)}) custom-call(bf16[768,128]{1,0:T(8,128)(2,1)S(1)} %fusion.17.q_ref, bf16[8,1536,128]{2,1,0:T(8,128)(2,1)S(1)} %copy-done.1, bf16[8,1536,128]{2,1,0:T(8,128)(2,1)S(1)} %copy-done.1, ...), custom_call_target="tpu_custom_call" | custom-call | tf_op jit(solution)/shard_map/attend_back/pallas_call | solution.py:560
  140.6 1.8 pad_maximum_fusion.refs_3_
  142.5 1.5 convolution_convert_fusion.3
  143.9 3.6 %convolution_convert_fusion.1 = bf16[3072,768]{1,0:T(8,128)(2,1)} fusion(bf16[128,3072]{1,0:T(8,128)(2,1)S(1)} %get-tuple-element.81, f32[128,768]{1,0:T(8,128)S(1)} %get-tuple-element.57), kind=kOutput, calls=%fused_computation.1 | convolution fusion | flops 606437376 | bytes 5898240 | tf_op jit(solution)/shard_map/dot_general | solution.py:38
  147.5 3.6 %convolution_convert_fusion.2 = bf16[768,3072]{1,0:T(8,128)(2,1)} fusion(bf16[128,3072]{1,0:T(8,128)(2,1)S(1)} %get-tuple-element.87, f32[128,768]{1,0:T(8,128)S(1)} %get-tuple-element.80, f32[768]{0:T(1024)S(1)} %reshape.228, f32[768]{0:T(1024)S(1)} %reshape.227, f32[128]{0:T(128)S(1)} %copy-done.16, f32[128]{0:T(128)S(1)} %broadcast_multiply_fusion.5), kind=kOutput, calls=%fused_computation.2 | convolution fusion | flops 606830592 | bytes 5905408 | tf_op jit(solution)/shard_map/dot_general | solution.py:38
  151.2 94.3 %scatter2.1 = (bf16[192,3072]{1,0:T(8,128)(2,1)}, bf16[768,768]{1,0:T(8,128)(2,1)}, bf16[192,768]{1,0:T(8,128)(2,1)}, f32[1536,128]{1,0:T(8,128)}) custom-call(bf16[4,192,3072]{2,1,0:T(8,128)(2,1)} %bitcast.51, bf16[4,768,768]{2,1,0:T(8,128)(2,1)} %bitcast.50, bf16[4,192,768]{2,1,0:T(8,128)(2,1)} %bitcast.63, bf16[8,1536,128]{2,1,0:T(8,128)(2,1)} %pad_maximum_fusion.refs_3_), custom_call_target="tpu_custom_call" | custom-call | tf_op jit(solution)/shard_map/scatter2/pallas_call | solution.py:477
  248.6 2.9 convolution_convert_fusion
  251.5 50.0 %scatter3.1 = (bf16[192,2304]{1,0:T(8,128)(2,1)}, bf16[32,256]{1,0:T(8,128)(2,1)}) custom-call(bf16[4,192,2304]{2,1,0:T(8,128)(2,1)} %bitcast.54, bf16[4,32,256]{2,1,0:T(8,128)(2,1)} %bitcast.64), custom_call_target="tpu_custom_call" | custom-call | tf_op jit(solution)/shard_map/scatter3/pallas_call | solution.py:477
  301.5 2.6 convert_element_type.283
  305.4 1.7 convert_element_type.287
  307.1 1.6 convert_element_type.288
  308.6 1.3 copy-done.2
  309.9 2.0 fusion.7
  (102 shorter events, 12.8 us)
Async XLA Ops:
  93.7 1.9 copy-start
  95.6 9.1 %copy-start.3 = (bf16[4,192,768]{2,1,0:T(8,128)(2,1)S(1)}, bf16[4,192,768]{2,1,0:T(8,128)(2,1)}, u32[]{:S(2)}) copy-start(bf16[4,192,768]{2,1,0:T(8,128)(2,1)} %get-tuple-element.36) | copy-start | bytes 3538948
  95.6 9.1 %copy-start.5 = (bf16[1,128,768]{2,1,0:T(8,128)(2,1)S(1)}, bf16[1,128,768]{2,1,0:T(8,128)(2,1)}, u32[]{:S(2)}) copy-start(bf16[1,128,768]{2,1,0:T(8,128)(2,1)} %param.16) | copy-start | bytes 589828
  105.4 7.9 %copy-start.15 = (f32[128]{0:T(128)}, f32[128]{0:T(128)S(1)}, u32[]{:S(2)}) copy-start(f32[128]{0:T(128)S(1)} %add_rsqrt_fusion.1) | copy-start | bytes 1540
  113.3 3.5 %copy-start.14 = (f32[4,192]{1,0:T(4,128)S(1)}, f32[4,192]{1,0:T(4,128)}, u32[]{:S(2)}) copy-start(f32[4,192]{1,0:T(4,128)} %get-tuple-element.63) | copy-start | bytes 9220
  113.3 3.6 %copy-start.7 = (bf16[1,128,768]{2,1,0:T(8,128)(2,1)S(1)}, bf16[1,128,768]{2,1,0:T(8,128)(2,1)}, u32[]{:S(2)}) copy-start(bf16[1,128,768]{2,1,0:T(8,128)(2,1)} %param.18) | copy-start | bytes 589828
  113.3 4.3 %copy-start.13 = (f32[4,192]{1,0:T(4,128)S(1)}, f32[4,192]{1,0:T(4,128)}, u32[]{:S(2)}) copy-start(f32[4,192]{1,0:T(4,128)} %get-tuple-element.64) | copy-start | bytes 9220
  117.7 9.5 %slice-start = ((s8[4718592]{0:T(1024)(128)(4,1)}), s8[4194304]{0:T(1024)(128)(4,1)S(1)}, s32[]{:S(2)}) async-start(s8[4718592]{0:T(1024)(128)(4,1)} %bitcast.56), calls=%async_computation | async-start | bytes 8388608
  119.1 8.1 %slice-start.1 = ((s8[4718592]{0:T(1024)(128)(4,1)}), s8[524288]{0:T(1024)(128)(4,1)S(1)}, s32[]{:S(2)}) async-start(s8[4718592]{0:T(1024)(128)(4,1)} %bitcast.56), calls=%async_computation.1 | async-start | bytes 1048576
  119.1 8.1 %copy-start.16 = (f32[128]{0:T(128)S(1)}, f32[128]{0:T(128)}, u32[]{:S(2)}) copy-start(f32[128]{0:T(128)} %copy-done.15) | copy-start | bytes 1540
  127.2 3.2 %copy-start.4 = (bf16[4,192,768]{2,1,0:T(8,128)(2,1)S(1)}, bf16[4,192,768]{2,1,0:T(8,128)(2,1)}, u32[]{:S(2)}) copy-start(bf16[4,192,768]{2,1,0:T(8,128)(2,1)} %get-tuple-element.36) | copy-start | bytes 3538948
  129.6 1.9 copy-start.1
  151.2 96.0 %copy-start.21 = (bf16[768]{0:T(1024)(128)(2,1)S(1)}, bf16[768]{0:T(1024)(128)(2,1)}, u32[]{:S(2)}) copy-start(bf16[768]{0:T(1024)(128)(2,1)} %get-tuple-element.58) | copy-start | bytes 4612
  151.2 96.1 %copy-start.20 = (bf16[768]{0:T(1024)(128)(2,1)S(1)}, bf16[768]{0:T(1024)(128)(2,1)}, u32[]{:S(2)}) copy-start(bf16[768]{0:T(1024)(128)(2,1)} %get-tuple-element.49) | copy-start | bytes 4612
  151.2 96.2 %copy-start.19 = (bf16[768]{0:T(1024)(128)(2,1)S(1)}, bf16[768]{0:T(1024)(128)(2,1)}, u32[]{:S(2)}) copy-start(bf16[768]{0:T(1024)(128)(2,1)} %get-tuple-element.54) | copy-start | bytes 4612
  151.2 96.3 %copy-start.22 = (bf16[3072]{0:T(1024)(128)(2,1)S(1)}, bf16[3072]{0:T(1024)(128)(2,1)}, u32[]{:S(2)}) copy-start(bf16[3072]{0:T(1024)(128)(2,1)} %get-tuple-element.86) | copy-start | bytes 18436
  151.2 96.3 %copy-start.18 = (bf16[768]{0:T(1024)(128)(2,1)S(1)}, bf16[768]{0:T(1024)(128)(2,1)}, u32[]{:S(2)}) copy-start(bf16[768]{0:T(1024)(128)(2,1)} %get-tuple-element.56) | copy-start | bytes 4612
  151.2 96.4 %copy-start.17 = (bf16[768]{0:T(1024)(128)(2,1)S(1)}, bf16[768]{0:T(1024)(128)(2,1)}, u32[]{:S(2)}) copy-start(bf16[768]{0:T(1024)(128)(2,1)} %get-tuple-element.51) | copy-start | bytes 4612
  151.2 96.5 %copy-start.8 = (bf16[1,128,768]{2,1,0:T(8,128)(2,1)S(1)}, bf16[1,128,768]{2,1,0:T(8,128)(2,1)}, u32[]{:S(2)}) copy-start(bf16[1,128,768]{2,1,0:T(8,128)(2,1)} %param.18) | copy-start | bytes 589828
  245.6 3.0 copy-start.6
  301.5 2.6 copy-start.12
  301.5 3.9 %copy-start.10 = (bf16[192,3072]{1,0:T(8,128)(2,1)S(1)}, bf16[192,3072]{1,0:T(8,128)(2,1)}, u32[]{:S(2)}) copy-start(bf16[192,3072]{1,0:T(8,128)(2,1)} %get-tuple-element.47) | copy-start | bytes 3538948
  307.1 2.9 copy-start.2
  309.9 2.0 copy-start.11
  (1 other events, 1.7 us)

commit v2 on v1

--- a/solution.py
+++ b/solution.py
@@ -201,10 +201,13 @@
     return list(outs)
 
 
-def add_into(dst, sources, rows, cols, chunk=16):
+def add_into(dst, sources, rows, cols):
+    fits = [k for k in range(16, rows + 1, 16) if rows % k == 0 and k * cols <= 24576]
+    chunk = max(fits) if fits else 16
+
     def view(item, r):
         ref, lead, row0, col0 = item
-        start = pl.multiple_of(row0 + r * chunk, chunk)
+        start = pl.multiple_of(row0 + r * chunk, 16)
         return ref.at[lead + (pl.ds(start, chunk), pl.ds(col0, cols))]
 
     def step(r, carry):
@@ -240,13 +243,6 @@
         across = [(s, above), (s, below)]
     greet([(here.right, c), (here.left, c), sib] + across)
 
-    offsets = []
-    for k in range(1, n // 2 + 1):
-        for o in (-k, k):
-            if o % n not in [q % n for q in offsets]:
-                offsets.append(o)
-    offsets.append(0)
-
     def half_rows(i):
         return ins[i].shape[1] // 2
 
@@ -256,13 +252,21 @@
     def theirs(i):
         return pl.multiple_of((1 - core) * half_rows(i), half_rows(i))
 
-    def swap(i, j):
-        block = here.at(offsets[j])
-        k = i * n + j
+    def region(k, d):
+        i, piece, width = units[k]
+        return i, half_rows(i), d * (ins[i].shape[2] // 2) + piece * width, width
+
+    def reach(d, j):
+        return here.at(-1 - j if d == 0 else 1 + j)
+
+    def swap(k, d, j):
+        i, rows, col, width = region(k, d)
+        block = reach(d, j)
+        q = (k * 2 + d) * n + j
         return remote(
-            ins[i].at[block, pl.ds(theirs(i), half_rows(i)), :],
-            got[i].at[block],
-            gsend.at[k], grecv.at[k], sib,
+            ins[i].at[block, pl.ds(theirs(i), rows), pl.ds(col, width)],
+            got[i].at[block, :, pl.ds(col, width)],
+            gsend.at[q], grecv.at[q], sib,
         )
 
     if kv:
@@ -280,30 +284,22 @@
                 mate.at[q], far.at[k - 1], ksend.at[k - 1], krecv.at[k - 1], across[k - 1]
             )
 
-        for k in list(range(1, pairs)) + [0]:
-            kv_swap(k).start()
-    for j in range(n):
-        for i in range(nw):
-            swap(i, j).start()
-    if kv:
-        for k in list(range(1, pairs)) + [0]:
+        def kv_step(k):
             q = lax.rem(m + k, pairs)
             kv_swap(k).wait_recv()
             add_into((mate, (q,), 0, 0), [(mate, (q,), 0, 0), (din, (q * 2 + core,), 0, 0)],
                      token_rows, token_cols)
             if k:
                 kv_send(k).start()
-    for j in range(n):
-        block = here.at(offsets[j])
-        for i in range(nw):
-            swap(i, j).wait_recv()
-            add_into((acc[i], (block,), 0, 0),
-                     [(got[i], (block,), 0, 0), (ins[i], (block,), mine(i), 0)],
-                     half_rows(i), ins[i].shape[2])
-
-    def region(k, d):
-        i, piece, width = units[k]
-        return i, half_rows(i), d * (ins[i].shape[2] // 2) + piece * width, width
+
+    kv_order = list(range(1, pairs)) + [0] if kv else []
+    swaps = sorted((k + j, k, j) for k in range(len(units)) for j in range(n))
+    for rank, (tick, k, j) in enumerate(swaps):
+        if rank == min(3, len(swaps) - 1):
+            for b in kv_order:
+                kv_swap(b).start()
+        for d in range(2):
+            swap(k, d, j).start()
 
     def ring(k, d, t):
         i, rows, col, width = region(k, d)
@@ -346,11 +342,13 @@
 
     def ring_step(t, k, d):
         i, rows, col, width = region(k, d)
+        block = reach(d, t + 1)
+        swap(k, d, t + 1).wait_recv()
+        items = [(got[i], (block,), 0, col), (ins[i], (block,), mine(i), col)]
         if t >= 0:
             ring(k, d, t).wait_recv()
-            block = here.at(-2 - t if d == 0 else 2 + t)
-            add_into((acc[i], (block,), 0, col), [(acc[i], (block,), 0, col), (hop[i], (t,), 0, col)],
-                     rows, width)
+            items.append((hop[i], (t,), 0, col))
+        add_into((acc[i], (block,), 0, col), items, rows, width)
         if t + 1 < n - 1:
             ring(k, d, t + 1).start()
 
@@ -417,6 +415,8 @@
             if 0 <= k < len(units):
                 for d in range(2):
                     stages[stage](k, d)
+        if tick < len(kv_order):
+            kv_step(kv_order[tick])
 
     if kv:
         items = [(mate, (m,), 0, 0)]
@@ -428,9 +428,10 @@
             kv_swap(k).wait_send()
             if k:
                 kv_send(k).wait_send()
-    for i in range(nw):
-        for j in range(n):
-            swap(i, j).wait_send()
+    for k in range(len(units)):
+        for d in range(2):
+            for j in range(n):
+                swap(k, d, j).wait_send()
     for k in range(len(units)):
         for d in range(2):
             for t in range(n - 1):
@@ -467,7 +468,7 @@
     scratch += [vm(h, BF16) for h in halves] * 2
     dma = pltpu.SemaphoreType.DMA
     both = 2 * len(units)
-    sems = [dma((nw * n,))] * 2 + [dma((both * (n - 1),))] * 2 + [dma((both,))] * 3
+    sems = [dma((both * n,))] * 2 + [dma((both * (n - 1),))] * 2 + [dma((both,))] * 3
     sems += [dma((2 * both,)), dma((both,)), dma((both,)), dma((both,))]
     if kv is not None:
         args.append(kv)
@@ -607,18 +608,18 @@
     limit = lengths[0]
     vectors = (b_query, b_value, b_out, ln1_gain, ln1_bias, b_down, ln2_gain, ln2_bias, b_up)
     lens = [v.shape[0] for v in vectors]
-    flat = jnp.concatenate(vectors)
     lane = 256
     rows = -(-sum(lens) // lane)
     rows = -(-rows // 32) * 32
-    flat = jnp.pad(flat, (0, rows * lane - sum(lens))).reshape(rows, lane)
+    base = min(lens)
+    flat = jnp.concatenate([v.astype(F32).reshape(-1, base) for v in vectors])
+    flat = jnp.pad(flat, ((0, -flat.shape[0] % 8), (0, -base % 128)))
     wq_all, small_all = gather(n, pairs, 0, [w_qkv], small=flat)
     wq_full = wq_all.reshape(width, -1)
-    small_all = small_all.reshape(n, rows * lane)
     parts, at = [], 0
     for size in lens:
-        parts.append(small_all[:, at : at + size].reshape(-1).astype(F32))
-        at += size
+        parts.append(small_all[:, at : at + size // base, :base].reshape(-1))
+        at += size // base
     bq, bv, bo, g1, c1, bd, g2, c2, bu = parts
 
     qkv_t = contract_dims(wq_full, x, 0, 1)

time: 313 us -> 308 us (0.984)
  Pallas kernels: 242 us -> 236 us
    pallas_call x2, Pallas kernels: 144 us -> 138 us  [scatter(): pl.pallas_call(functools.partial(scatter_kernel, n, pairs, nw, tuple(unit...]
    concatenate x1 -> x2, local copies, waits for them, and re-layouts: 6.1 us -> 0.05 us  [the longest x1 0.04 us: local(): flat = jnp.concatenate([v.astype(F32).reshape(-1, base) for v in vectors])]
    reshape x1 -> x10, local copies, waits for them, and re-layouts: 0.62 us -> 6.11 us  [the longest x9 6.03 us: local(): flat = jnp.concatenate([v.astype(F32).reshape(-1, base) for v in vectors])]
where the time goes in v2:
time: 308 us
  Pallas kernels  236 us (77%)
  matrix products  39.2 us (13%)
  local copies, waits for them, and re-layouts  15.9 us (5%)
  other arithmetic  15.3 us (5%)
    pallas_call x2, Pallas kernels, scatter(): pl.pallas_call(functools.partial(scatter_kernel, n, pairs, nw, tuple(unit...  138 us
    pallas_call x2, Pallas kernels, gather(): pl.pallas_call(functools.partial(gather_kernel, n, pairs, nw, small is no...  79.6 us
    dot_general x10, matrix products, contract_dims(): lax.dot_general(left, right, (((left_dim,), (right_dim,)), ((), ())), pre...  28.3 us
    pallas_call x1, Pallas kernels, attend_back(): pl.pallas_call(functools.partial(attend_back_kernel, scale), grid=(HEADS,...  9.12 us
    pallas_call x1, Pallas kernels, attend(): pl.pallas_call(functools.partial(attend_kernel, scale), grid=(HEADS,), ou...  9 us
    dot_general x1, matrix products, local(): upper = jnp.dot(x_one_b, wu_full, preferred_element_type=F32) + bu  7.59 us

profile of v2, /device:TPU:0, one launch (start us, length us, event | category | flops | bytes accessed | tf_op | source)
XLA Modules:
  0.0 307.6 jit_solution(18325050335877127854)
XLA Ops:
  7.3 25.0 %gather0.1 = (bf16[4,192,2304]{2,1,0:T(8,128)(2,1)}, f32[4,16,256]{2,1,0:T(8,128)}) custom-call(bf16[192,2304]{1,0:T(8,128)(2,1)} %refs_0_.2, f32[16,256]{1,0:T(8,128)} %pad_convert_fusion.refs_1_), custom_call_target="tpu_custom_call" | custom-call | tf_op jit(solution)/shard_map/gather0/pallas_call | solution.py:187
  32.3 1.9 slice_reduce_fusion.2
  34.4 3.1 %fusion.23 = f32[2304,128]{1,0:T(8,128)S(1)} fusion(bf16[768,2304]{1,0:T(8,128)(2,1)} %bitcast.50, bf16[1,128,768]{2,1,0:T(8,128)(2,1)} %param.16), kind=kOutput, calls=%fused_computation.60 | convolution fusion | flops 452984832 | bytes 4915200 | tf_op jit(solution)/shard_map/dot_general | solution.py:38
  38.5 54.6 %gather1.1 = (bf16[4,192,768]{2,1,0:T(8,128)(2,1)}, bf16[4,192,3072]{2,1,0:T(8,128)(2,1)}, bf16[4,768,768]{2,1,0:T(8,128)(2,1)}, bf16[8,1536,128]{2,1,0:T(8,128)(2,1)}) custom-call(bf16[192,768]{1,0:T(8,128)(2,1)} %refs_0_.3, bf16[192,3072]{1,0:T(8,128)(2,1)} %refs_1_.1, bf16[768,768]{1,0:T(8,128)(2,1)} %refs_2_.1, bf16[1536,128]{1,0:T(8,128)(2,1)} %fusion.9.refs_3_), custom_call_target="tpu_custom_call" | custom-call | tf_op jit(solution)/shard_map/gather1/pallas_call | solution.py:187
  94.0 1.9 copy-done
  95.9 9.0 %attend.1 = (f32[768,128]{1,0:T(8,128)S(1)}, f32[12,128,1]{2,1,0:T(8,128)S(1)}) custom-call(bf16[768,128]{1,0:T(8,128)(2,1)S(1)} %fusion.17.q_ref, bf16[8,1536,128]{2,1,0:T(8,128)(2,1)S(1)} %copy-done, bf16[8,1536,128]{2,1,0:T(8,128)(2,1)S(1)} %copy-done, f32[1,1024]{1,0:T(1,128)S(1)} %compare_convert_fusion.valid_ref), custom_call_target="tpu_custom_call" | custom-call | tf_op jit(solution)/shard_map/attend/pallas_call | solution.py:511
  106.7 7.6 %multiply_convert_fusion = (bf16[128,3072]{1,0:T(8,128)(2,1)S(1)}, f32[128,3072]{1,0:T(8,128)}) fusion(f32[3072]{0:T(1024)S(1)} %add.115, bf16[768,3072]{1,0:T(8,128)(2,1)} %bitcast.53, f32[128,768]{1,0:T(8,128)S(1)} %get-tuple-element.80, f32[768]{0:T(1024)S(1)} %add.112, f32[768]{0:T(1024)S(1)} %mul.127, f32[128]{0:T(128)S(1)} %add_rsqrt_fusion.1, ...), kind=kOutput, calls=%fused_computation.8 | convolution fusion | flops 630423552 | bytes 7490560 | tf_op jit(solution)/shard_map/dot_general | solution.py:641
  114.4 3.3 %fusion.45 = (f32[128]{0:T(128)S(1)}, f32[128,768]{1,0:T(8,128)S(1)}) fusion(f32[768]{0:T(1024)S(1)} %add.119, bf16[128,3072]{1,0:T(8,128)(2,1)S(1)} %get-tuple-element.81, bf16[3072,768]{1,0:T(8,128)(2,1)} %bitcast.57, f32[768]{0:T(1024)S(1)} %add.112, f32[768]{0:T(1024)S(1)} %mul.127, f32[128]{0:T(128)S(1)} %add_rsqrt_fusion.1, ...), kind=kOutput, calls=%fused_computation.97 | convolution fusion | flops 604667776 | bytes 6302208 | tf_op jit(solution)/shard_map/dot_general | solution.py:644
  118.8 1.5 fusion.39
  120.3 8.1 %fusion.46 = (bf16[3072]{0:T(1024)(128)(2,1)}, bf16[128,3072]{1,0:T(8,128)(2,1)S(1)}) fusion(f32[128,3072]{1,0:T(8,128)} %get-tuple-element.82, bf16[3072,768]{1,0:T(8,128)(2,1)} %bitcast.58, f32[128,768]{1,0:T(8,128)S(1)} %get-tuple-element.65), kind=kOutput, calls=%fused_computation.98 | convolution fusion | flops 632779776 | bytes 7477248 | tf_op jit(solution)/shard_map/dot_general | solution.py:38
  128.4 2.4 multiply_reduce_fusion
  132.6 9.1 %attend_back.1 = (f32[768,128]{1,0:T(8,128)S(1)}, bf16[8,768,128]{2,1,0:T(8,128)(2,1)S(1)}, bf16[8,768,128]{2,1,0:T(8,128)(2,1)S(1)}) custom-call(bf16[768,128]{1,0:T(8,128)(2,1)S(1)} %fusion.17.q_ref, bf16[8,1536,128]{2,1,0:T(8,128)(2,1)S(1)} %copy-done.1, bf16[8,1536,128]{2,1,0:T(8,128)(2,1)S(1)} %copy-done.1, ...), custom_call_target="tpu_custom_call" | custom-call | tf_op jit(solution)/shard_map/attend_back/pallas_call | solution.py:561
  141.8 1.8 pad_maximum_fusion.refs_3_
  143.6 1.5 convolution_convert_fusion.3
  145.1 3.6 %convolution_convert_fusion.1 = bf16[3072,768]{1,0:T(8,128)(2,1)} fusion(bf16[128,3072]{1,0:T(8,128)(2,1)S(1)} %get-tuple-element.81, f32[128,768]{1,0:T(8,128)S(1)} %get-tuple-element.65), kind=kOutput, calls=%fused_computation.1 | convolution fusion | flops 606437376 | bytes 5898240 | tf_op jit(solution)/shard_map/dot_general | solution.py:38
  148.7 3.6 %convolution_convert_fusion.2 = bf16[768,3072]{1,0:T(8,128)(2,1)} fusion(bf16[128,3072]{1,0:T(8,128)(2,1)S(1)} %get-tuple-element.87, f32[128,768]{1,0:T(8,128)S(1)} %get-tuple-element.80, f32[768]{0:T(1024)S(1)} %add.112, f32[768]{0:T(1024)S(1)} %mul.127, f32[128]{0:T(128)S(1)} %copy-done.16, f32[128]{0:T(128)S(1)} %broadcast_multiply_fusion.5), kind=kOutput, calls=%fused_computation.2 | convolution fusion | flops 606830592 | bytes 5905408 | tf_op jit(solution)/shard_map/dot_general | solution.py:38
  152.4 89.8 %scatter2.1 = (bf16[192,3072]{1,0:T(8,128)(2,1)}, bf16[768,768]{1,0:T(8,128)(2,1)}, bf16[192,768]{1,0:T(8,128)(2,1)}, f32[1536,128]{1,0:T(8,128)}) custom-call(bf16[4,192,3072]{2,1,0:T(8,128)(2,1)} %bitcast.49, bf16[4,768,768]{2,1,0:T(8,128)(2,1)} %bitcast.48, bf16[4,192,768]{2,1,0:T(8,128)(2,1)} %bitcast.61, bf16[8,1536,128]{2,1,0:T(8,128)(2,1)} %pad_maximum_fusion.refs_3_), custom_call_target="tpu_custom_call" | custom-call | tf_op jit(solution)/shard_map/scatter2/pallas_call | solution.py:478
  245.2 2.9 convolution_convert_fusion
  248.1 48.1 %scatter3.1 = (bf16[192,2304]{1,0:T(8,128)(2,1)}, bf16[32,256]{1,0:T(8,128)(2,1)}) custom-call(bf16[4,192,2304]{2,1,0:T(8,128)(2,1)} %bitcast.52, bf16[4,32,256]{2,1,0:T(8,128)(2,1)} %bitcast.62), custom_call_target="tpu_custom_call" | custom-call | tf_op jit(solution)/shard_map/scatter3/pallas_call | solution.py:478
  296.3 2.6 convert_element_type.191
  300.2 1.7 convert_element_type.195
  301.8 1.6 convert_element_type.196
  303.4 1.3 copy-done.2
  304.7 2.0 fusion.7
  (109 shorter events, 18.1 us)
Async XLA Ops:
  94.0 1.9 copy-start
  95.9 9.1 %copy-start.3 = (bf16[4,192,768]{2,1,0:T(8,128)(2,1)S(1)}, bf16[4,192,768]{2,1,0:T(8,128)(2,1)}, u32[]{:S(2)}) copy-start(bf16[4,192,768]{2,1,0:T(8,128)(2,1)} %get-tuple-element.36) | copy-start | bytes 3538948
  95.9 9.1 %copy-start.5 = (bf16[1,128,768]{2,1,0:T(8,128)(2,1)S(1)}, bf16[1,128,768]{2,1,0:T(8,128)(2,1)}, u32[]{:S(2)}) copy-start(bf16[1,128,768]{2,1,0:T(8,128)(2,1)} %param.16) | copy-start | bytes 589828
  105.7 8.7 %copy-start.15 = (f32[128]{0:T(128)}, f32[128]{0:T(128)S(1)}, u32[]{:S(2)}) copy-start(f32[128]{0:T(128)S(1)} %add_rsqrt_fusion.1) | copy-start | bytes 1540
  114.4 3.5 %copy-start.14 = (f32[4,192]{1,0:T(4,128)S(1)}, f32[4,192]{1,0:T(4,128)}, u32[]{:S(2)}) copy-start(f32[4,192]{1,0:T(4,128)} %get-tuple-element.56) | copy-start | bytes 9220
  114.4 3.6 %copy-start.7 = (bf16[1,128,768]{2,1,0:T(8,128)(2,1)S(1)}, bf16[1,128,768]{2,1,0:T(8,128)(2,1)}, u32[]{:S(2)}) copy-start(bf16[1,128,768]{2,1,0:T(8,128)(2,1)} %param.18) | copy-start | bytes 589828
  114.4 4.3 %copy-start.13 = (f32[4,192]{1,0:T(4,128)S(1)}, f32[4,192]{1,0:T(4,128)}, u32[]{:S(2)}) copy-start(f32[4,192]{1,0:T(4,128)} %get-tuple-element.57) | copy-start | bytes 9220
  118.8 9.5 %slice-start = ((s8[4718592]{0:T(1024)(128)(4,1)}), s8[4194304]{0:T(1024)(128)(4,1)S(1)}, s32[]{:S(2)}) async-start(s8[4718592]{0:T(1024)(128)(4,1)} %bitcast.54), calls=%async_computation | async-start | bytes 8388608
  120.3 8.1 %slice-start.1 = ((s8[4718592]{0:T(1024)(128)(4,1)}), s8[524288]{0:T(1024)(128)(4,1)S(1)}, s32[]{:S(2)}) async-start(s8[4718592]{0:T(1024)(128)(4,1)} %bitcast.54), calls=%async_computation.1 | async-start | bytes 1048576
  120.3 8.1 %copy-start.16 = (f32[128]{0:T(128)S(1)}, f32[128]{0:T(128)}, u32[]{:S(2)}) copy-start(f32[128]{0:T(128)} %copy-done.15) | copy-start | bytes 1540
  128.3 3.2 %copy-start.4 = (bf16[4,192,768]{2,1,0:T(8,128)(2,1)S(1)}, bf16[4,192,768]{2,1,0:T(8,128)(2,1)}, u32[]{:S(2)}) copy-start(bf16[4,192,768]{2,1,0:T(8,128)(2,1)} %get-tuple-element.36) | copy-start | bytes 3538948
  130.7 1.9 copy-start.1
  152.3 91.5 %copy-start.21 = (bf16[768]{0:T(1024)(128)(2,1)S(1)}, bf16[768]{0:T(1024)(128)(2,1)}, u32[]{:S(2)}) copy-start(bf16[768]{0:T(1024)(128)(2,1)} %get-tuple-element.66) | copy-start | bytes 4612
  152.3 91.6 %copy-start.20 = (bf16[768]{0:T(1024)(128)(2,1)S(1)}, bf16[768]{0:T(1024)(128)(2,1)}, u32[]{:S(2)}) copy-start(bf16[768]{0:T(1024)(128)(2,1)} %get-tuple-element.49) | copy-start | bytes 4612
  152.3 91.7 %copy-start.19 = (bf16[768]{0:T(1024)(128)(2,1)S(1)}, bf16[768]{0:T(1024)(128)(2,1)}, u32[]{:S(2)}) copy-start(bf16[768]{0:T(1024)(128)(2,1)} %get-tuple-element.54) | copy-start | bytes 4612
  152.3 91.8 %copy-start.22 = (bf16[3072]{0:T(1024)(128)(2,1)S(1)}, bf16[3072]{0:T(1024)(128)(2,1)}, u32[]{:S(2)}) copy-start(bf16[3072]{0:T(1024)(128)(2,1)} %get-tuple-element.86) | copy-start | bytes 18436
  152.3 91.8 %copy-start.18 = (bf16[768]{0:T(1024)(128)(2,1)S(1)}, bf16[768]{0:T(1024)(128)(2,1)}, u32[]{:S(2)}) copy-start(bf16[768]{0:T(1024)(128)(2,1)} %get-tuple-element.64) | copy-start | bytes 4612
  152.3 91.9 %copy-start.17 = (bf16[768]{0:T(1024)(128)(2,1)S(1)}, bf16[768]{0:T(1024)(128)(2,1)}, u32[]{:S(2)}) copy-start(bf16[768]{0:T(1024)(128)(2,1)} %get-tuple-element.51) | copy-start | bytes 4612
  152.3 91.9 %copy-start.8 = (bf16[1,128,768]{2,1,0:T(8,128)(2,1)S(1)}, bf16[1,128,768]{2,1,0:T(8,128)(2,1)}, u32[]{:S(2)}) copy-start(bf16[1,128,768]{2,1,0:T(8,128)(2,1)} %param.18) | copy-start | bytes 589828
  242.2 3.0 copy-start.6
  296.3 2.6 copy-start.12
  296.3 3.9 %copy-start.10 = (bf16[192,3072]{1,0:T(8,128)(2,1)S(1)}, bf16[192,3072]{1,0:T(8,128)(2,1)}, u32[]{:S(2)}) copy-start(bf16[192,3072]{1,0:T(8,128)(2,1)} %get-tuple-element.47) | copy-start | bytes 3538948
  301.8 2.9 copy-start.2
  304.7 2.0 copy-start.11
  (1 other events, 1.7 us)
